TPU v7x, 32 devices: a whole 2x2x4 slice. The times are simulated.
32 devices in a mesh: tier: 16 (over z, x, core), sys: 2 (over y).
Axes of the slice: x: 2, y: 2, z: 4, core: 2. Of those that a mesh axis runs over, the one named last changes fastest.
Arguments:
- state: float32 [64, 2, 512, 512], P('tier', None, 'sys'), may hold values from -6 to 6
- slope: float32 [64, 2, 512, 512], P('tier', None, 'sys'), may hold values from -6 to 6
- counts: int32 [16], replicated, may hold values from 1 to 4, 32 in all
- links: int32 [4, 64, 24], P(None, 'tier'), may hold values from 0 to 63, as said below
- mode_site: int32 [12], replicated, may hold values from 0 to 511, as said below
- mode_coef: float32 [2, 12], replicated, may hold values from -3 to 3
- mode_rate: float32 [12], replicated, may hold values from 0.01 to 0.1
- h_bands: float32 [9, 512], replicated, may hold values from -3 to 3
Outputs:
- slope_next: float32 [64, 2, 512, 512], P('tier', None, 'sys')
- partial_sum: float32 [64, 2, 512, 512], P('tier', None, 'sys')
Inputs may be any that keep to these rules, and one draw needn't show every extreme that they name: Index d of tier holds counts[d] live auxiliary operators, in its first slots; the counts sum to 32. links[0] is a global slot (index of tier times 4 plus the slot), links[1] a mode below 12, links[2] is 0 or 1, links[3] is 1 or 2. Each slot has exactly one link with direction 0 and one with direction 1 for every mode. Of the 96 links of the slots of one index of tier, exactly 6 name slots of each index of tier; of the links whose mode k has k // 6 equal to one row block's number, at most 4 name slots of one index of tier, and in every row block some index of tier is named by exactly 4 of them. `mode_site`: mode k's site lies in row block k // 6, that is in rows (k // 6) * 256 to (k // 6) * 256 + 255; the sites are distinct.
All inputs are finite; a program needn't handle non-finite values.
Results may differ from a plain program's by a relative error of at most 0.0003.
Values sent between devices are 32-bit elements; how exact they have to be, the bound alone decides.
A program may use at most 64 MiB of HBM per device.

v0:
```python
import jax
import jax.numpy as jnp
from jax import lax
from jax.sharding import PartitionSpec as P

step_size = 0.05


def padded_2(block, sides, width):
    for axis, dim in sides:
        count = lax.axis_size(axis)
        forward = [(i, i + 1) for i in range(count - 1)]
        backward = [(target, source) for source, target in forward]
        low = lax.ppermute(
            lax.slice_in_dim(block, block.shape[dim] - width, None, axis=dim), axis, forward
        )
        high = lax.ppermute(lax.slice_in_dim(block, 0, width, axis=dim), axis, backward)
        block = jnp.concatenate([low, block, high], axis=dim)
    return block


def lookup(index, table):
    matches = index[..., None] == jnp.arange(table.shape[-1], dtype=jnp.int32)
    return jnp.sum(jnp.where(matches, table, jnp.zeros((), table.dtype)), axis=-1)


def shifted_band(h_bands):
    band_width = h_bands.shape[0] - 1
    length = h_bands.shape[1]
    padded = jnp.pad(h_bands, ((0, 0), (band_width, 0)))
    return jnp.stack(
        [
            padded[offset, band_width - offset : band_width - offset + length]
            for offset in range(band_width + 1)
        ]
    )


def band_rows(padded, upper_band, lower_band, band_width):
    length = upper_band.shape[1]
    summed = upper_band[0][:, None] * padded[..., band_width : band_width + length, :]
    for offset in range(1, band_width + 1):
        summed = (
            summed
            + upper_band[offset][:, None]
            * padded[..., band_width + offset : band_width + offset + length, :]
        )
        summed = (
            summed
            + lower_band[offset][:, None]
            * padded[..., band_width - offset : band_width - offset + length, :]
        )
    return summed


def band_cols(field, upper_band, lower_band, band_width):
    length = field.shape[-1]
    padded = jnp.pad(field, ((0, 0),) * (field.ndim - 1) + ((band_width, band_width),))
    summed = upper_band[0] * field
    for offset in range(1, band_width + 1):
        summed = (
            summed
            + upper_band[offset] * padded[..., band_width + offset : band_width + offset + length]
        )
        summed = (
            summed
            + lower_band[offset] * padded[..., band_width - offset : band_width - offset + length]
        )
    return summed


def shards(state, slope, counts, links, mode_site, mode_coef, mode_rate, h_bands):
    slot_count = state.shape[0]
    row_count = state.shape[2]
    levels = state.shape[3]
    band_width = h_bands.shape[0] - 1
    link_total = links.shape[1] * links.shape[2]
    per_slot = links.shape[2]
    mode_total = mode_site.shape[0]
    block_modes = mode_total // lax.axis_size("sys")
    tier_index = lax.axis_index("tier")
    sys_index = lax.axis_index("sys")
    row_start = sys_index * row_count
    midpoint = state + 0.5 * step_size * slope
    padded = padded_2(midpoint, (("sys", 2),), band_width)
    neighbour = links[0].reshape(-1)
    link_mode = links[1].reshape(-1)
    link_kind = links[2].reshape(-1)
    link_level = links[3].reshape(-1).astype(jnp.float32)
    sites_of = lookup(link_mode, mode_site)
    holder = neighbour // slot_count
    target_slot = neighbour % slot_count
    in_block = link_mode // block_modes == sys_index
    local_row = jnp.clip(sites_of - row_start, 0, row_count - 1)
    neighbour_live = (target_slot < lookup(holder, counts)).astype(jnp.float32)
    downward = link_kind == 1
    weight_re = (
        jnp.where(downward, link_level * lookup(link_mode, mode_coef[0]), 1.0) * neighbour_live
    )
    weight_im = (
        jnp.where(downward, link_level * lookup(link_mode, mode_coef[1]), 0.0) * neighbour_live
    )
    rate_of = jnp.where(downward, link_level * lookup(link_mode, mode_rate), 0.0)
    damping = jnp.sum(rate_of.reshape(slot_count, per_slot), axis=1)
    packet_cols = jnp.transpose(midpoint[:, :, :, mode_site], (0, 3, 1, 2)).reshape(
        slot_count, mode_total, 2 * row_count
    )
    block_sites = (
        lax.dynamic_slice_in_dim(mode_site, sys_index * block_modes, block_modes) - row_start
    )
    packet_rows = jnp.transpose(midpoint[:, :, block_sites, :], (0, 2, 1, 3)).reshape(
        slot_count, block_modes, 2 * levels
    )
    local_mode = jnp.clip(link_mode - sys_index * block_modes, 0, block_modes - 1)
    piece_cols = lax.all_gather(packet_cols, "tier", axis=0, tiled=True)
    piece_rows = lax.all_gather(packet_rows, "tier", axis=0, tiled=True)
    length = piece_cols.shape[0]
    inside = (neighbour >= 0) & (neighbour < length)
    clipped = jnp.clip(neighbour, 0, length - 1)
    sum_cols = jnp.where(inside[:, None], piece_cols[clipped, link_mode], 0.0)
    sum_rows = jnp.where((inside & in_block)[:, None], piece_rows[clipped, local_mode], 0.0)
    column_part = sum_cols
    row_part = sum_rows
    lower_full = shifted_band(h_bands)
    upper_local = lax.dynamic_slice_in_dim(h_bands, row_start, row_count, 1)
    lower_local = lax.dynamic_slice_in_dim(lower_full, row_start, row_count, 1)
    commuted = band_rows(padded, upper_local, lower_local, band_width) - band_cols(
        midpoint, h_bands, lower_full, band_width
    )
    deriv_re = commuted[:, 1] - damping[:, None, None] * midpoint[:, 0]
    deriv_im = -commuted[:, 0] - damping[:, None, None] * midpoint[:, 1]
    column_part = column_part.reshape(link_total, 2, row_count)
    row_part = row_part.reshape(link_total, 2, levels)
    col_re = -(weight_re[:, None] * column_part[:, 1] - weight_im[:, None] * column_part[:, 0])
    col_im = weight_re[:, None] * column_part[:, 0] + weight_im[:, None] * column_part[:, 1]
    row_re = jnp.where(
        in_block[:, None],
        weight_re[:, None] * row_part[:, 1] + weight_im[:, None] * row_part[:, 0],
        0.0,
    )
    row_im = jnp.where(
        in_block[:, None],
        -(weight_re[:, None] * row_part[:, 0] - weight_im[:, None] * row_part[:, 1]),
        0.0,
    )
    col_pair = jnp.stack([col_re, col_im], axis=1).reshape(slot_count, per_slot, 2, row_count)
    row_pair = jnp.stack([row_re, row_im], axis=1).reshape(slot_count, per_slot, 2, levels)
    site_table = (
        (sites_of[:, None] == jnp.arange(levels, dtype=jnp.int32)[None, :])
        .astype(jnp.float32)
        .reshape(slot_count, per_slot, levels)
    )
    row_table = (
        (local_row[:, None] == jnp.arange(row_count, dtype=jnp.int32)[None, :])
        .astype(jnp.float32)
        .reshape(slot_count, per_slot, row_count)
    )
    added_cols = jnp.einsum("gkcr,gkl->gcrl", col_pair, site_table, precision=lax.Precision.HIGHEST)
    added_rows = jnp.einsum("gkr,gkcl->gcrl", row_table, row_pair, precision=lax.Precision.HIGHEST)
    live = (jnp.arange(slot_count, dtype=jnp.int32) < lookup(tier_index, counts)).astype(
        jnp.float32
    )
    slope_next = (jnp.stack([deriv_re, deriv_im], axis=1) + added_cols + added_rows) * live[
        :, None, None, None
    ]
    partial_sum = (state + step_size / 6.0 * slope + step_size / 3.0 * slope_next) * live[
        :, None, None, None
    ]
    return (slope_next, partial_sum)


def solution(mesh):
    in_specs = (
        P("tier", None, "sys", None),
        P("tier", None, "sys", None),
        P(),
        P(None, "tier", None),
        P(),
        P(),
        P(),
        P(),
    )
    out_specs = (P("tier", None, "sys", None), P("tier", None, "sys", None))
    return jax.shard_map(shards, mesh=mesh, in_specs=in_specs, out_specs=out_specs, check_vma=False)
```

profile of v0, /device:TPU:11, one launch (start us, length us, event | category | flops | bytes accessed | tf_op | source)
XLA Modules:
  0.0 138.8 jit_solution(12746841936256002478)
XLA Ops:
  7.2 0.0 all-gather.3.cloned.1.call-start
  7.2 0.7 compare_select_fusion.4
  7.9 6.5 %multiply_add_fusion = f32[4,2,256,512]{3,2,1,0:T(8,128)} fusion(f32[4,2,256,512]{3,2,1,0:T(8,128)} %param.8, f32[4,2,256,512]{3,2,1,0:T(8,128)} %param.9), kind=kLoop, calls=%fused_computation.129 | loop fusion | flops 2097152 | bytes 12582912 | tf_op jit(solution)/shard_map/add | solution.py:84
  14.4 5.3 %copy.36 = f32[4,2,256,512]{2,0,3,1:T(4,128)} copy(f32[4,2,256,512]{3,2,1,0:T(8,128)} %multiply_add_fusion) | data formatting | bytes 8388608 | tf_op jit(solution)/shard_map/add | solution.py:84
  19.7 2.8 %gather_fusion = f32[12,4,2,256]{3,1,2,0:T(4,128)S(1)} fusion(f32[4,2,256,512]{2,0,3,1:T(4,128)} %copy.36, s32[1024]{0:T(1024)S(1)} %pad_clamp_fusion.1), kind=kCustom, calls=%fused_computation | custom fusion | bytes 196656 | tf_op jit(solution)/shard_map/gather | solution.py:105
  22.5 0.7 copy.37
  23.1 0.0 all-gather.3.cloned.1.call-update
  23.2 0.0 all-gather.5.cloned.1.call-start
  23.2 1.0 fusion.116
  24.2 1.3 collective-permute-start
  25.5 4.0 %collective-permute-start.1 = (f32[4,2,8,512]{3,2,1,0:T(8,128)S(1)}, f32[4,2,8,512]{3,2,1,0:T(8,128)S(1)}, u32[]{:S(2)}, u32[]{:S(2)}) collective-permute-start(f32[4,2,8,512]{3,2,1,0:T(8,128)S(1)} %get-tuple-element.14), channel_id=1, source_target_pairs={{0,1},{2,3},{4,5},{6,7},{8,9},{10,11},{12,13},{14,15},{16,17},{18,... | collective-permute-start | bytes 393224 | tf_op jit(solution)/shard_map/ppermute | solution.py:14
  29.5 0.0 copy-start.7
  29.5 0.0 copy-start.4
  29.5 0.0 copy-start.5
  29.6 0.0 copy-start.8
  29.6 0.0 copy-start.6
  29.6 0.0 copy-start.3
  29.6 6.9 %copy.40 = f32[4,2,256,512]{3,0,2,1:T(4,128)} copy(f32[4,2,256,512]{3,2,1,0:T(8,128)} %multiply_add_fusion) | data formatting | bytes 8388608 | tf_op jit(solution)/shard_map/add | solution.py:84
  36.5 0.0 copy-done.7
  36.5 0.1 compare_select_fusion.1
  36.6 2.8 %gather_fusion.2 = f32[6,4,2,512]{3,1,2,0:T(4,128)S(1)} fusion(f32[4,2,256,512]{3,0,2,1:T(4,128)} %copy.40, s32[1024]{0:T(1024)S(1)} %pad_clamp_fusion), kind=kCustom, calls=%fused_computation.2 | custom fusion | bytes 196632 | tf_op jit(solution)/shard_map/gather | solution.py:111
  39.4 0.7 copy.41
  40.1 0.0 all-gather.5.cloned.1.call-update
  40.2 0.0 copy-done.4
  40.2 0.1 eq.125
  40.3 0.1 reshape_squeeze.9
  40.4 0.1 reshape_squeeze.8
  40.4 0.1 select_reduce_fusion
  40.6 0.0 copy-done.5
  40.6 0.1 convert_element_type.33
  40.7 0.0 copy-done.8
  40.7 0.7 fusion.99
  41.4 0.1 select_reduce_fusion.3
  41.5 0.1 min.24
  41.5 0.1 eq.133
  41.6 0.1 select_reduce_fusion.4
  41.7 0.1 reduce_sum.66
  41.8 0.1 fusion.97
  41.9 0.1 eq.132
  42.0 0.0 copy-done.3
  42.0 0.1 fusion.118
  42.2 0.7 compare_convert_fusion
  42.9 0.1 stack.26
  42.9 0.1 constant_dynamic-slice_fusion
  43.0 0.0 collective-permute-done
  43.1 0.0 collective-permute-done.1
  43.1 0.0 copy-start
  43.1 67.2 %fusion.17 = f32[4,2,256,512]{3,2,1,0:T(8,128)S(1)} fusion(f32[4,2,256,512]{3,2,1,0:T(8,128)} %multiply_add_fusion, f32[4,2,8,512]{3,2,1,0:T(8,128)S(1)} %collective-permute-done.1, f32[4,2,8,512]{3,2,1,0:T(8,128)S(1)} %collective-permute-done, f32[512]{0:T(512)S(1)} %bitcast.95, f32[512]{0:T(512)S(1)} %bitcast.103, f32[512]{0:T(512)S(1)} %bitcast.94, ...), kind=kLoop, calls=%fused_computation.51 | loop fusion | flops 87031808 | bytes 8702976 | tf_op jit(solution)/shard_map/sub | solution.py:127
  110.3 3.1 %fusion.82 = (f32[4,1,256,512]{3,2,1,0:T(8,128)}, f32[4,1,256,512]{3,2,1,0:T(8,128)}) fusion(f32[4,2,256,512]{3,2,1,0:T(8,128)S(1)} %copy-done, f32[4,2,256,512]{3,2,1,0:T(8,128)S(1)} %fusion.17, f32[4]{0:T(128)S(1)} %get-tuple-element.7), kind=kLoop, calls=%fused_computation.134 | loop fusion | flops 2621440 | bytes 12582928 | tf_op jit(solution)/shard_map/sub | solution.py:130
  113.4 2.5 %copy.38 = f32[64,12,512]{2,0,1:T(8,128)S(1)} copy(f32[64,12,512]{2,1,0:T(8,128)} %all-gather.3.cloned.1.call-done) | data formatting | bytes 3145728 | tf_op jit(solution)/shard_map/all_gather | solution.py:115
  115.9 1.4 %gather_fusion.1 = f32[96,512]{1,0:T(8,128)S(1)} fusion(f32[64,12,512]{2,0,1:T(8,128)S(1)} %copy.38, s32[96]{0:T(128)S(1)} %get-tuple-element.58), kind=kCustom, calls=%fused_computation.1 | custom fusion | bytes 393984 | tf_op jit(solution)/shard_map/gather | solution.py:120
  117.4 0.1 bitcast_select_fusion.1
  117.5 0.0 all-gather.5.cloned.1.call-done
  117.5 2.5 %copy.42 = f32[64,6,1024]{2,0,1:T(8,128)S(1)} copy(f32[64,6,1024]{2,1,0:T(8,128)} %all-gather.5.cloned.1.call-done) | data formatting | bytes 3145728 | tf_op jit(solution)/shard_map/all_gather | solution.py:116
  120.0 1.6 %gather_fusion.3 = f32[96,1024]{1,0:T(8,128)S(1)} fusion(f32[64,6,1024]{2,0,1:T(8,128)S(1)} %copy.42, s32[96]{0:T(128)S(1)} %get-tuple-element.57), kind=kCustom, calls=%fused_computation.3 | custom fusion | bytes 787200 | tf_op jit(solution)/shard_map/gather | solution.py:121
  121.6 0.0 copy-start.1
  121.6 0.0 copy-start.2
  121.6 0.1 bitcast_select_fusion
  121.7 0.1 subtract_negate_fusion
  121.8 0.1 add_select_fusion
  122.0 1.9 %fusion.86 = f32[4,2,256,512]{3,2,1,0:T(8,128)S(1)} fusion(f32[4,24,1,256]{3,1,2,0:T(8,128)S(1)} %bitcast.87, f32[4,24,1,256]{3,1,2,0:T(8,128)S(1)} %bitcast.86, s32[4,24]{1,0:T(4,128)S(1)} %eq.133), kind=kOutput, calls=%fused_computation.140 | convolution fusion | flops 302088192 | bytes 4391296 | tf_op jit(solution)/shard_map/gkcr,gkl->gcrl/dot_general | solution.py:158
  123.8 0.0 copy-done.1
  123.9 0.6 copy-done.2
  124.5 7.5 %add_multiply_fusion = (f32[4,2,256,512]{3,2,1,0:T(8,128)}, f32[4,2,256,512]{3,2,1,0:T(8,128)}) fusion(f32[4,2,256,512]{3,2,1,0:T(8,128)S(1)} %copy-done.1, f32[4,2,256,512]{3,2,1,0:T(8,128)} %param.9, f32[4]{0:T(128)S(1)} %compare_convert_fusion, s32[4,24]{1,0:T(4,128)S(1)} %subtract_clamp_fusion, f32[4,24,1,512]{3,1,2,0:T(8,128)S(1)} %bitcast.83, ...), kind=kOutput, calls=%fused_computation.128 | convolution fusion | flops 311549952 | bytes 25559440 | tf_op jit(solution)/shard_map/gkr,gkcl->gcrl/dot_general | solution.py:159
  (13 shorter events, 0.1 us)
Async XLA Ops:
  7.2 106.3 %all-gather.3.cloned.1.call-start = ((), (), s32[]{:S(2)}) async-start(), calls=%async_computation | async-start | bytes 2228224 | tf_op jit(solution)/shard_map/all_gather | solution.py:115
  23.2 94.3 %all-gather.5.cloned.1.call-start = ((), (), s32[]{:S(2)}) async-start(), calls=%async_computation.1 | async-start | bytes 2228224 | tf_op jit(solution)/shard_map/all_gather | solution.py:116
  24.2 18.8 %collective-permute-start = (f32[4,2,8,512]{3,2,1,0:T(8,128)S(1)}, f32[4,2,8,512]{3,2,1,0:T(8,128)S(1)}, u32[]{:S(2)}, u32[]{:S(2)}) collective-permute-start(f32[4,2,8,512]{3,2,1,0:T(8,128)S(1)} %get-tuple-element.13), channel_id=1, source_target_pairs={{1,0},{3,2},{5,4},{7,6},{9,8},{11,10},{13,12},{15,14},{17,16},{19,... | collective-permute-start | bytes 393224 | tf_op jit(solution)/shard_map/ppermute | solution.py:17
  25.5 17.6 %collective-permute-start.1 = (f32[4,2,8,512]{3,2,1,0:T(8,128)S(1)}, f32[4,2,8,512]{3,2,1,0:T(8,128)S(1)}, u32[]{:S(2)}, u32[]{:S(2)}) collective-permute-start(f32[4,2,8,512]{3,2,1,0:T(8,128)S(1)} %get-tuple-element.14), channel_id=1, source_target_pairs={{0,1},{2,3},{4,5},{6,7},{8,9},{10,11},{12,13},{14,15},{16,17},{18,... | collective-permute-start | bytes 393224 | tf_op jit(solution)/shard_map/ppermute | solution.py:14
  29.5 7.0 %copy-start.7 = (s32[12]{0:T(128)S(1)}, s32[12]{0:T(128)}, u32[]{:S(2)}) copy-start(s32[12]{0:T(128)} %param.12) | copy-start | bytes 148
  29.5 10.6 %copy-start.4 = (s32[4,4,24]{2,1,0:T(4,128)S(1)}, s32[4,4,24]{2,1,0:T(4,128)}, u32[]{:S(2)}) copy-start(s32[4,4,24]{2,1,0:T(4,128)} %param.11) | copy-start | bytes 4612
  29.5 11.0 %copy-start.5 = (f32[2,12]{1,0:T(2,128)S(1)}, f32[2,12]{1,0:T(2,128)}, u32[]{:S(2)}) copy-start(f32[2,12]{1,0:T(2,128)} %param.13) | copy-start | bytes 292
  29.6 11.1 %copy-start.8 = (s32[16]{0:T(128)S(1)}, s32[16]{0:T(128)}, u32[]{:S(2)}) copy-start(s32[16]{0:T(128)} %param.10) | copy-start | bytes 196
  29.6 12.1 %copy-start.6 = (f32[12]{0:T(128)S(1)}, f32[12]{0:T(128)}, u32[]{:S(2)}) copy-start(f32[12]{0:T(128)} %param.14) | copy-start | bytes 148
  29.6 12.4 %copy-start.3 = (f32[9,512]{1,0:T(8,128)S(1)}, f32[9,512]{1,0:T(8,128)}, u32[]{:S(2)}) copy-start(f32[9,512]{1,0:T(8,128)} %param.15) | copy-start | bytes 55300
  43.1 67.2 %copy-start = (f32[4,2,256,512]{3,2,1,0:T(8,128)S(1)}, f32[4,2,256,512]{3,2,1,0:T(8,128)}, u32[]{:S(2)}) copy-start(f32[4,2,256,512]{3,2,1,0:T(8,128)} %multiply_add_fusion) | copy-start | bytes 12582916
  121.6 2.3 %copy-start.1 = (f32[4,2,256,512]{3,2,1,0:T(8,128)S(1)}, f32[4,2,256,512]{3,2,1,0:T(8,128)}, u32[]{:S(2)}) copy-start(f32[4,2,256,512]{3,2,1,0:T(8,128)} %param.8) | copy-start | bytes 12582916
  121.6 2.9 %copy-start.2 = (f32[4,1,256,512]{3,2,1,0:T(8,128)S(1)}, f32[4,1,256,512]{3,2,1,0:T(8,128)}, u32[]{:S(2)}) copy-start(f32[4,1,256,512]{3,2,1,0:T(8,128)} %get-tuple-element.11) | copy-start | bytes 6291460
Sparse Core Ops, SparseCore 0:
  23.3 41.0 all-gather.2
  67.1 40.1 all-gather.4
where the time goes:
time: 140 us; the launch traced here: 139 us
  other arithmetic  79.8 us (57%)
  local copies, waits for them, and re-layouts  29.8 us (21%)
  between operations  14.4 us (10%)
  matrix products  9.35 us (7%)
  starting transfers between devices  5.37 us (4%)
    sub x1, other arithmetic, shards(): band_rows(padded, upper_local, lower_local, band_width)  67.2 us
    add x2, local copies, waits for them, and re-layouts, shards(): midpoint = state + 0.5 * step_size * slope  12.2 us
    dot_general x1, matrix products, shards(): jnp.einsum('gkr,gkcl->gcrl', row_table, row_pair, precision=lax.Precision...  7.47 us
    add x1, other arithmetic, shards(): midpoint = state + 0.5 * step_size * slope  6.51 us
    ppermute x1, starting transfers between devices, padded_2(): lax.ppermute(lax.slice_in_dim(block, block.shape[dim] - width, None, axis...  4 us
    sub x1, other arithmetic, shards(): deriv_re = commuted[:, 1] - damping[:, None, None] * midpoint[:, 0]  3.09 us
    gather x1, local copies, waits for them, and re-layouts, shards(): midpoint[:, :, block_sites, :]  2.81 us
  transfers between devices with their start and end apart: 4, of which 0 were waited for; matrix products, arithmetic and copies ran while one was open for 64% of the time, Pallas kernels for 0%

commit v1 on v0

v1 whole, which is shorter than its diff:
```python
import functools

import jax
import jax.numpy as jnp
from jax import lax
from jax.experimental import pallas as pl
from jax.experimental.pallas import tpu as pltpu
from jax.sharding import PartitionSpec as P

step_size = 0.05
MESH = pl.DeviceIdType.MESH
f32 = jnp.float32
bf16 = jnp.bfloat16


def up(value, unit):
    return (value + unit - 1) // unit * unit


def split(value):
    hi = value.astype(bf16)
    lo = (value - hi.astype(f32)).astype(bf16)
    return hi, lo


def mm(a, b):
    return lax.dot_general(a, b, (((1,), (0,)), ((), ())), preferred_element_type=f32)


def mm_nt(a, b):
    return lax.dot_general(a, b, (((1,), (1,)), ((), ())), preferred_element_type=f32)


def mm3(a, b):
    a_hi, a_lo = split(a)
    b_hi, b_lo = split(b)
    return mm(a_hi, b_hi) + (mm(a_hi, b_lo) + mm(a_lo, b_hi))


def exchange_kernel(
    dims,
    req_ref,
    lane_ref,
    site_ref,
    damp_ref,
    neg_h_ref,
    loc_h_ref,
    halo_h_ref,
    mix_c_ref,
    mix_r_ref,
    state_hbm,
    slope_hbm,
    d_hbm,
    c_ref,
    r_ref,
    st,
    sl,
    z_hi,
    z_lo,
    d_buf,
    req_in,
    halo_st,
    halo_sl,
    col_acc,
    row_pack,
    sel_c,
    sel_r,
    send_c,
    send_r,
    recv_c,
    recv_r,
    load_sem,
    out_sem,
    req_send,
    req_recv,
    halo_send,
    halo_recv,
    c_send,
    c_recv,
    r_send,
    r_recv,
):
    tiers, systems, slots, modes, block, edge, cw, rw = dims
    rows, levels = st.shape[1], st.shape[2]
    me = lax.axis_index("tier")
    sy = lax.axis_index("sys")
    planes = slots * 2

    def load(p):
        g, c = p // 2, p % 2
        return (
            pltpu.make_async_copy(state_hbm.at[g, c], st.at[p], load_sem.at[0, p]),
            pltpu.make_async_copy(slope_hbm.at[g, c], sl.at[p], load_sem.at[1, p]),
        )

    for p in range(planes):
        for copy in load(p):
            copy.start()

    barrier = pltpu.get_barrier_semaphore()

    def greet(i, carry):
        pl.semaphore_signal(
            barrier, inc=1, device_id=(lax.rem(me + i, tiers), sy), device_id_type=MESH
        )
        return carry

    lax.fori_loop(1, tiers, greet, 0)

    @pl.when(sy > 0)
    def _():
        pl.semaphore_signal(barrier, inc=1, device_id=(me, sy - 1), device_id_type=MESH)

    @pl.when(sy < systems - 1)
    def _():
        pl.semaphore_signal(barrier, inc=1, device_id=(me, sy + 1), device_id_type=MESH)

    inner = (sy > 0).astype(jnp.int32) + (sy < systems - 1).astype(jnp.int32)
    pl.semaphore_wait(barrier, tiers - 1 + inner)

    def send(src, dst, send_sem, recv_sem, i):
        peer = lax.rem(me + i, tiers)
        return pltpu.make_async_remote_copy(
            src_ref=src.at[peer],
            dst_ref=dst.at[me],
            send_sem=send_sem.at[i],
            recv_sem=recv_sem.at[i],
            device_id=(peer, sy),
            device_id_type=MESH,
        )

    def receive(src, dst, send_sem, recv_sem, i):
        peer = lax.rem(me + tiers - i, tiers)
        return pltpu.make_async_remote_copy(
            src_ref=src.at[peer],
            dst_ref=dst.at[peer],
            send_sem=send_sem.at[i],
            recv_sem=recv_sem.at[i],
            device_id=(peer, sy),
            device_id_type=MESH,
        )

    def req_start(i, carry):
        send(req_ref, req_in, req_send, req_recv, i).start()
        return carry

    lax.fori_loop(1, tiers, req_start, 0)

    def halo(side):
        first = rows - edge if side == 0 else 0
        target = sy + 1 if side == 0 else sy - 1
        return [
            pltpu.make_async_remote_copy(
                src_ref=src.at[:, :, pl.ds(first, edge), :],
                dst_ref=dst.at[side],
                send_sem=halo_send.at[side, n],
                recv_sem=halo_recv.at[side, n],
                device_id=(me, target),
                device_id_type=MESH,
            )
            for n, (src, dst) in enumerate(((state_hbm, halo_st), (slope_hbm, halo_sl)))
        ]

    @pl.when(sy < systems - 1)
    def _():
        for copy in halo(0):
            copy.start()

    @pl.when(sy > 0)
    def _():
        for copy in halo(1):
            copy.start()

    @pl.when(sy == 0)
    def _():
        halo_st[0] = jnp.zeros_like(halo_st[0])
        halo_sl[0] = jnp.zeros_like(halo_sl[0])

    @pl.when(sy == systems - 1)
    def _():
        halo_st[1] = jnp.zeros_like(halo_st[1])
        halo_sl[1] = jnp.zeros_like(halo_sl[1])

    req_in[me] = req_ref[me]
    row_pack[...] = jnp.zeros_like(row_pack)
    width = col_acc.shape[-1]
    lane_site = lane_ref[0:1, :]
    lane_slot = lane_ref[1:2, :]
    level_at = lax.broadcasted_iota(jnp.int32, (levels, width), 0)
    for g in range(slots):
        pick = jnp.where((level_at == lane_site) & (lane_slot == g), 1.0, 0.0).astype(bf16)
        for c in range(2):
            p = g * 2 + c
            for copy in load(p):
                copy.wait()
            hi, lo = split(st[p] + (0.5 * step_size) * sl[p])
            z_hi[p] = hi
            z_lo[p] = lo
            col_hi = mm(hi, pick)
            col_lo = mm(lo, pick)
            if g == 0:
                col_acc[c] = col_hi
                col_acc[2 + c] = col_lo
            else:
                col_acc[c] += col_hi
                col_acc[2 + c] += col_lo
    for c in range(2):
        for g in range(slots):
            for k in range(block):
                at = site_ref[k]
                p = g * 2 + c
                row = st[p, pl.ds(at, 1), :] + (0.5 * step_size) * sl[p, pl.ds(at, 1), :]
                dest = (c * slots + g) * block + k
                row_pack[dest : dest + 1, :] = row

    def req_wait(i, carry):
        receive(req_ref, req_in, req_send, req_recv, i).wait_recv()
        return carry

    lax.fori_loop(1, tiers, req_wait, 0)
    codes = jnp.transpose(req_in[:, 0, :])
    lane_c = lax.broadcasted_iota(jnp.int32, (cw, sel_c.shape[1]), 1).astype(f32)
    lane_r = lax.broadcasted_iota(jnp.int32, (rw, sel_r.shape[1]), 1).astype(f32)
    for t in range(tiers):
        sel_c[t * cw : (t + 1) * cw, :] = jnp.where(codes[0:cw, t : t + 1] == lane_c, 1.0, 0.0)
        sel_r[t * rw : (t + 1) * rw, :] = jnp.where(
            codes[cw : cw + rw, t : t + 1] == lane_r, 1.0, 0.0
        )
    pick_c = sel_c[...].astype(bf16)
    pick_r = sel_r[...].astype(bf16)
    pack_hi, pack_lo = split(row_pack[...])
    send_r[...] = (mm(pick_r, pack_hi) + mm(pick_r, pack_lo)).reshape(tiers, rw, levels)
    for c in range(2):
        packed = mm_nt(pick_c, col_acc[c].astype(bf16)) + mm_nt(
            pick_c, col_acc[2 + c].astype(bf16)
        )
        send_c[:, :, c * rows : (c + 1) * rows] = packed.reshape(tiers, cw, rows)

    def pack_start(i, carry):
        send(send_r, recv_r, r_send, r_recv, i).start()
        send(send_c, recv_c, c_send, c_recv, i).start()
        return carry

    lax.fori_loop(1, tiers, pack_start, 0)
    recv_c[me] = send_c[me]
    recv_r[me] = send_r[me]

    @pl.when(sy > 0)
    def _():
        for copy in halo(0):
            copy.wait_recv()

    @pl.when(sy < systems - 1)
    def _():
        for copy in halo(1):
            copy.wait_recv()

    neg_hi, neg_lo = split(neg_h_ref[...])
    loc_hi, loc_lo = split(loc_h_ref[...])

    def commute(p):
        hi, lo = z_hi[p], z_lo[p]
        g, c = p // 2, p % 2
        both = mm(loc_hi, hi) + mm(hi, neg_hi)
        both += mm(loc_hi, lo) + mm(hi, neg_lo)
        both += mm(loc_lo, hi) + mm(lo, neg_hi)
        ghost = [halo_st[s, g, c] + (0.5 * step_size) * halo_sl[s, g, c] for s in range(2)]
        extra = mm3(halo_h_ref[...], jnp.concatenate(ghost, axis=0))
        return both, extra

    for g in range(slots):
        for c in range(2):
            both, extra = commute(g * 2 + 1 - c)
            p = g * 2 + c
            sign = 1.0 if c == 0 else -1.0
            mid = st[p] + (0.5 * step_size) * sl[p]
            d_buf[p] = sign * both - damp_ref[g] * mid
            d_buf[p, 0:edge, :] += sign * extra[0:edge]
            d_buf[p, rows - edge : rows, :] += sign * extra[edge : 2 * edge]
            pltpu.make_async_copy(d_buf.at[p], d_hbm.at[g, c], out_sem.at[p]).start()

    def pack_wait(i, carry):
        receive(send_r, recv_r, r_send, r_recv, i).wait_recv()
        receive(send_c, recv_c, c_send, c_recv, i).wait_recv()
        return carry

    lax.fori_loop(1, tiers, pack_wait, 0)
    got_c = recv_c[...].reshape(tiers * cw, 2 * rows)
    got_r = recv_r[...].reshape(tiers * rw, levels)
    r_ref[...] = mm3(mix_r_ref[...], got_r)
    c_ref[...] = mm3(mix_c_ref[0], got_c[:, 0:rows]) + mm3(mix_c_ref[1], got_c[:, rows : 2 * rows])

    def finish(i, carry):
        send(req_ref, req_in, req_send, req_recv, i).wait_send()
        send(send_r, recv_r, r_send, r_recv, i).wait_send()
        send(send_c, recv_c, c_send, c_recv, i).wait_send()
        return carry

    lax.fori_loop(1, tiers, finish, 0)

    @pl.when(sy < systems - 1)
    def _():
        for copy in halo(0):
            copy.wait_send()

    @pl.when(sy > 0)
    def _():
        for copy in halo(1):
            copy.wait_send()

    for p in range(planes):
        pltpu.make_async_copy(d_buf.at[p], d_hbm.at[p // 2, p % 2], out_sem.at[p]).wait()


def finish_kernel(
    live_ref, col_site_ref, row_site_ref, c_ref, r_ref, d_ref, st_ref, sl_ref, next_ref, sum_ref
):
    rows, levels = d_ref.shape[2], d_ref.shape[3]
    wide_m, wide_b = c_ref.shape[0], r_ref.shape[0]
    live = live_ref[pl.program_id(0)]
    lanes = lax.broadcasted_iota(jnp.int32, (wide_m, levels), 1)
    spread = jnp.where(col_site_ref[...] == lanes, 1.0, 0.0).astype(bf16)
    row_lanes = lax.broadcasted_iota(jnp.int32, (wide_b, rows), 1)
    row_at = jnp.where(row_site_ref[...] == row_lanes, 1.0, 0.0)
    col = c_ref[...]
    col_hi = col.astype(bf16).astype(f32)
    left = jnp.concatenate([col_hi, col - col_hi, row_at, row_at], axis=0)
    row_hi, row_lo = split(r_ref[...])
    right = jnp.concatenate([spread, spread, row_hi, row_lo], axis=0)
    added = mm(jnp.transpose(left).astype(bf16), right)
    slope_next = (d_ref[0, 0] + added) * live
    next_ref[0, 0] = slope_next
    sum_ref[0, 0] = (
        st_ref[0, 0] + step_size / 6.0 * sl_ref[0, 0] + step_size / 3.0 * slope_next
    ) * live


def lookup(index, table):
    matches = index[..., None] == jnp.arange(table.shape[-1], dtype=jnp.int32)
    return jnp.sum(jnp.where(matches, table, jnp.zeros((), table.dtype)), axis=-1)


def shards(tiers, systems, state, slope, counts, links, mode_site, mode_coef, mode_rate, h_bands):
    slots, _, rows, levels = state.shape
    edge = h_bands.shape[0] - 1
    modes = mode_site.shape[0]
    block = modes // systems
    per_slot = links.shape[2]
    total = slots * per_slot
    cp = total // tiers
    rp = 2 * -(-(slots * block) // tiers)
    cw, rw = up(cp, 8), up(2 * rp, 8)
    wide_m, wide_b = up(modes, 16), up(block, 16)
    tier_index = lax.axis_index("tier")
    sys_index = lax.axis_index("sys")
    row_start = sys_index * rows

    neighbour = links[0].reshape(-1)
    mode = links[1].reshape(-1)
    downward = links[2].reshape(-1) == 1
    level = links[3].reshape(-1).astype(f32)
    holder = neighbour // slots
    target = neighbour % slots
    in_block = mode // block == sys_index
    local_mode = mode - sys_index * block
    near = (target < lookup(holder, counts)).astype(f32)
    w_re = jnp.where(downward, level * lookup(mode, mode_coef[0]), 1.0) * near
    w_im = jnp.where(downward, level * lookup(mode, mode_coef[1]), 0.0) * near
    rate = jnp.where(downward, level * lookup(mode, mode_rate), 0.0)
    damp = jnp.sum(rate.reshape(slots, per_slot), axis=1)
    order = jnp.arange(total, dtype=jnp.int32)
    same = (holder[:, None] == holder[None, :]) & (order[None, :] < order[:, None])
    rank_c = jnp.sum(same.astype(jnp.int32), axis=1)
    rank_r = jnp.sum((same & in_block[None, :]).astype(jnp.int32), axis=1)

    lane = jnp.arange(128, dtype=jnp.int32)
    here = holder[None, :] == jnp.arange(tiers, dtype=jnp.int32)[:, None]
    code_c = target * modes + mode
    hit = here[:, None, :] & (rank_c[None, None, :] == lane[None, :, None])
    req = jnp.sum(jnp.where(hit, (code_c + 1)[None, None, :], 0), axis=-1)
    for c in range(2):
        hit = (
            here[:, None, :]
            & (in_block & (rank_r < rp))[None, None, :]
            & ((cw + c * rp + rank_r)[None, None, :] == lane[None, :, None])
        )
        code_r = (c * slots + target) * block + local_mode
        req += jnp.sum(jnp.where(hit, (code_r + 1)[None, None, :], 0), axis=-1)
    req = (req - 1).astype(f32).reshape(tiers, 1, 128)

    wide_gm = up(slots * modes, 128)
    lane_gm = jnp.arange(wide_gm, dtype=jnp.int32)
    lane_site = jnp.where(
        lane_gm < slots * modes, jnp.pad(jnp.tile(mode_site, slots), (0, wide_gm - slots * modes)), -1
    )
    lane_info = jnp.stack([lane_site, lane_gm // modes])
    block_sites = lax.dynamic_slice_in_dim(mode_site, sys_index * block, block) - row_start

    slot_of = order // per_slot
    gck = jnp.arange(slots * 2 * wide_m, dtype=jnp.int32)
    g_i, c_i, k_i = gck // (2 * wide_m), gck // wide_m % 2, gck % wide_m
    owns = (g_i[:, None] == slot_of[None, :]) & (k_i[:, None] == mode[None, :])
    at_c = (
        (holder * cw + rank_c)[:, None] == jnp.arange(tiers * cw, dtype=jnp.int32)[None, :]
    ).astype(f32)
    first = (c_i == 0)[:, None]
    coef_from_re = jnp.where(owns, jnp.where(first, w_im[None, :], w_re[None, :]), 0.0)
    coef_from_im = jnp.where(owns, jnp.where(first, -w_re[None, :], w_im[None, :]), 0.0)
    hp = lax.Precision.HIGHEST
    mix_c = jnp.dot(
        jnp.concatenate([coef_from_re, coef_from_im]), at_c, precision=hp
    ).reshape(2, slots * 2 * wide_m, tiers * cw)
    gck = jnp.arange(slots * 2 * wide_b, dtype=jnp.int32)
    g_i, c_i, k_i = gck // (2 * wide_b), gck // wide_b % 2, gck % wide_b
    owns = (
        (g_i[:, None] == slot_of[None, :])
        & (k_i[:, None] == local_mode[None, :])
        & in_block[None, :]
    )
    first = (c_i == 0)[:, None]
    packet_r = jnp.arange(tiers * rw, dtype=jnp.int32)[None, :]
    at_re = ((holder * rw + rank_r)[:, None] == packet_r).astype(f32)
    at_im = ((holder * rw + rp + rank_r)[:, None] == packet_r).astype(f32)
    row_from_re = jnp.where(owns, jnp.where(first, w_im[None, :], -w_re[None, :]), 0.0)
    row_from_im = jnp.where(owns, jnp.where(first, w_re[None, :], w_im[None, :]), 0.0)
    mix_r = jnp.dot(
        jnp.concatenate([row_from_re, row_from_im], axis=1),
        jnp.concatenate([at_re, at_im], axis=0),
        precision=hp,
    )

    i_at = jnp.arange(levels, dtype=jnp.int32)[:, None]
    j_at = jnp.arange(levels, dtype=jnp.int32)[None, :]
    shifted = jnp.pad(h_bands, ((0, 0), (edge, 0)))
    dense = jnp.zeros((levels, levels), f32)
    for o in range(edge + 1):
        dense = jnp.where(i_at - j_at == o, h_bands[o][None, :], dense)
        if o:
            dense = jnp.where(
                j_at - i_at == o, shifted[o, edge - o : edge - o + levels][None, :], dense
            )
    local = lax.dynamic_slice(dense, (row_start, row_start), (rows, rows))
    padded = jnp.pad(dense, ((0, 0), (edge, edge)))
    top = lax.dynamic_slice(padded, (row_start, row_start), (edge, edge))
    bottom = lax.dynamic_slice(
        padded, (row_start + rows - edge, row_start + rows + edge), (edge, edge)
    )
    blank = jnp.zeros((edge, edge), f32)
    halo_h = jnp.concatenate(
        [jnp.concatenate([top, blank], axis=1), jnp.concatenate([blank, bottom], axis=1)], axis=0
    )

    vmem = pl.BlockSpec(memory_space=pltpu.VMEM)
    smem = pl.BlockSpec(memory_space=pltpu.SMEM)
    hbm = pl.BlockSpec(memory_space=pl.ANY)
    planes = slots * 2
    wide_rp = up(2 * slots * block, 128)
    dma = pltpu.SemaphoreType.DMA
    deriv, col_mix, row_mix = pl.pallas_call(
        functools.partial(
            exchange_kernel, (tiers, systems, slots, modes, block, edge, cw, rw)
        ),
        out_shape=(
            jax.ShapeDtypeStruct(state.shape, f32),
            jax.ShapeDtypeStruct((slots * 2 * wide_m, rows), f32),
            jax.ShapeDtypeStruct((slots * 2 * wide_b, levels), f32),
        ),
        in_specs=[vmem, vmem, smem, smem, vmem, vmem, vmem, vmem, vmem, hbm, hbm],
        out_specs=(hbm, vmem, vmem),
        scratch_shapes=[
            pltpu.VMEM((planes, rows, levels), f32),
            pltpu.VMEM((planes, rows, levels), f32),
            pltpu.VMEM((planes, rows, levels), bf16),
            pltpu.VMEM((planes, rows, levels), bf16),
            pltpu.VMEM((planes, rows, levels), f32),
            pltpu.VMEM((tiers, 1, 128), f32),
            pltpu.VMEM((2, slots, 2, edge, levels), f32),
            pltpu.VMEM((2, slots, 2, edge, levels), f32),
            pltpu.VMEM((4, rows, wide_gm), f32),
            pltpu.VMEM((wide_rp, levels), f32),
            pltpu.VMEM((tiers * cw, wide_gm), f32),
            pltpu.VMEM((tiers * rw, wide_rp), f32),
            pltpu.VMEM((tiers, cw, 2 * rows), f32),
            pltpu.VMEM((tiers, rw, levels), f32),
            pltpu.VMEM((tiers, cw, 2 * rows), f32),
            pltpu.VMEM((tiers, rw, levels), f32),
            dma((2, planes)),
            dma((planes,)),
            dma((tiers,)),
            dma((tiers,)),
            dma((2, 2)),
            dma((2, 2)),
            dma((tiers,)),
            dma((tiers,)),
            dma((tiers,)),
            dma((tiers,)),
        ],
        compiler_params=pltpu.CompilerParams(collective_id=0, has_side_effects=True),
        name="exchange",
    )(req, lane_info, block_sites, damp, -dense, local, halo_h, mix_c, mix_r, state, slope)

    live = (jnp.arange(slots, dtype=jnp.int32) < lookup(tier_index, counts)).astype(f32)
    col_site = jnp.pad(mode_site, (0, wide_m - modes), constant_values=-1)[:, None]
    row_site = jnp.pad(block_sites, (0, wide_b - block), constant_values=-1)[:, None]
    plane = pl.BlockSpec((1, 1, rows, levels), lambda g, c: (g, c, 0, 0))
    fixed = lambda g, c: (0, 0)
    mixed = lambda g, c: (g * 2 + c, 0)
    return pl.pallas_call(
        finish_kernel,
        grid=(slots, 2),
        out_shape=(jax.ShapeDtypeStruct(state.shape, f32),) * 2,
        in_specs=[
            smem,
            pl.BlockSpec((wide_m, 1), fixed),
            pl.BlockSpec((wide_b, 1), fixed),
            pl.BlockSpec((wide_m, rows), mixed),
            pl.BlockSpec((wide_b, levels), mixed),
            plane,
            plane,
            plane,
        ],
        out_specs=(plane, plane),
        name="finish",
    )(live, col_site, row_site, col_mix, row_mix, deriv, state, slope)


def solution(mesh):
    in_specs = (
        P("tier", None, "sys", None),
        P("tier", None, "sys", None),
        P(),
        P(None, "tier", None),
        P(),
        P(),
        P(),
        P(),
    )
    out_specs = (P("tier", None, "sys", None), P("tier", None, "sys", None))
    body = functools.partial(shards, mesh.shape["tier"], mesh.shape["sys"])
    return jax.shard_map(body, mesh=mesh, in_specs=in_specs, out_specs=out_specs, check_vma=False)
```

time: 140 us -> 56.6 us (0.40)
  other arithmetic: 79.8 us -> 11.9 us
  Pallas kernels: 0 us -> 35.4 us
  local copies, waits for them, and re-layouts: 29.8 us -> 6.11 us
  between operations: 14.4 us -> 0.76 us
  matrix products: 9.35 us -> 1.81 us
  starting transfers between devices: 5.37 us -> 0 us
    sub x2 -> x1, other arithmetic: 70.3 us -> 0.74 us  [shards(): lax.dynamic_slice_in_dim(mode_site, sys_index * block, block) - row_start]
    pallas_call x0 -> x2, Pallas kernels: none -> 35.4 us  [the longest x1 24.4 us: shards(): pl.pallas_call(functools.partial(exchange_kernel, (tiers, systems, slots,...]
    add x2 -> x0, local copies, waits for them, and re-layouts: 12.2 us -> none  [shards(): midpoint = state + 0.5 * step_size * slope]
    gather x4 -> x0, local copies, waits for them, and re-layouts: 8.62 us -> none  [the longest x1 2.81 us: shards(): midpoint[:, :, block_sites, :]]
    dot_general x2, matrix products: 9.35 us -> 1.81 us  [the longest x1 0.92 us: shards(): jnp.dot(jnp.concatenate([coef_from_re, coef_from_im]), at_c, precision=hp)]
    add x1 -> x3, other arithmetic: 6.51 us -> 0.03 us  [the longest x2 0.02 us: shards(): req += jnp.sum(jnp.where(hit, (code_r + 1)[None, None, :], 0), axis=-1)]
    ppermute x2 -> x0, starting transfers between devices: 5.29 us -> none  [the longest x1 4 us: padded_2(): lax.ppermute(lax.slice_in_dim(block, block.shape[dim] - width, None, axis...]
    all_gather x2 -> x0, local copies, waits for them, and re-layouts: 5.01 us -> none  [the longest x1 2.51 us: shards(): piece_rows = lax.all_gather(packet_rows, 'tier', axis=0, tiled=True)]
  transfers between devices with their start and end apart: 4 -> 0, of which waited for: 0 -> 0; matrix products, arithmetic and copies ran while one was open for 64% -> 0% of each run, Pallas kernels for 0% -> 0%
where the time goes in v1:
time: 56.6 us; the launch traced here: 55.9 us
  Pallas kernels  35.4 us (63%)
  other arithmetic  11.9 us (21%)
  local copies, waits for them, and re-layouts  6.11 us (11%)
  matrix products  1.81 us (3%)
  between operations  0.76 us (1%)
    pallas_call x1, Pallas kernels, shards(): pl.pallas_call(functools.partial(exchange_kernel, (tiers, systems, slots,...  24.4 us
    pallas_call x1, Pallas kernels, shards(): pl.pallas_call(finish_kernel, grid=(slots, 2), out_shape=(jax.ShapeDtypeS...  11 us
    reduce_sum x3, other arithmetic, lookup(): jnp.sum(jnp.where(matches, table, jnp.zeros((), table.dtype)), axis=-1)  2.78 us
    select_n x1, other arithmetic, shards(): jnp.where(j_at - i_at == o, shifted[o, edge - o:edge - o + levels][None,...  1.47 us
    reduce_sum x1, other arithmetic, shards(): damp = jnp.sum(rate.reshape(slots, per_slot), axis=1)  1.39 us
    slice x1, local copies, waits for them, and re-layouts, shards(): shifted[o, edge - o:edge - o + levels][None, :]  1.37 us
    broadcast_in_dim x2, local copies, waits for them, and re-layouts, shards(): jnp.pad(mode_site, (0, wide_m - modes), constant_values=-1)[:, None]  1.34 us
    convert_element_type x1, other arithmetic, shards(): (jnp.arange(slots, dtype=jnp.int32) < lookup(tier_index, counts)).astype(...  1.24 us

profile of v1, /device:TPU:11, one launch (start us, length us, event | category | flops | bytes accessed | tf_op | source)
XLA Modules:
  0.0 55.9 jit_solution(3205064472752749958)
XLA Ops:
  0.6 0.7 %dynamic-slice_subtract_fusion.site_ref = s32[6]{0:T(128)S(1)} fusion(s32[12]{0:T(128)} %param.12, s32[]{:T(128)S(6)} %select_n.285, s32[]{:T(128)S(6)} %mul.71), kind=kLoop, calls=%fused_computation.122 | loop fusion | flops 6 | bytes 56 | tf_op jit(solution)/shard_map/sub | solution.py:397
  1.4 0.0 copy-start
  1.4 1.3 %fusion.33 = s32[]{:T(128)} fusion(s32[16]{0:T(128)} %param.10, s32[]{:T(128)S(6)} %axis_index.23), kind=kLoop, calls=%fused_computation.106 | loop fusion | flops 47 | bytes 72 | tf_op jit(solution)/shard_map/reduce_sum | solution.py:340
  2.7 1.2 %compare_convert_fusion.live_ref = f32[4]{0:T(128)} fusion(s32[]{:T(128)} %fusion.33), kind=kLoop, calls=%fused_computation.92 | loop fusion | flops 8 | bytes 20 | tf_op jit(solution)/shard_map/convert_element_type | solution.py:502
  3.9 0.7 %pad_bitcast_fusion.1 = s32[16,1]{0,1:T(1,128)S(1)} fusion(s32[12]{0:T(128)} %param.12), kind=kLoop, calls=%fused_computation.123 | loop fusion | bytes 112 | tf_op jit(solution)/shard_map/broadcast_in_dim | solution.py:503
  4.6 0.8 %slice_bitcast_fusion = (f32[12]{0:T(128)S(1)}, f32[12]{0:T(128)S(1)}) fusion(f32[2,12]{1,0:T(2,128)} %param.13), kind=kLoop, calls=%fused_computation.112 | loop fusion | bytes 192 | tf_op jit(solution)/shard_map/squeeze | solution.py:367
  5.4 0.7 %tile.4 = s32[4,12]{1,0:T(4,128)S(1)} broadcast(s32[12]{0:T(128)} %param.12), dimensions={1} | broadcast | bytes 240 | tf_op jit(solution)/shard_map/tile | solution.py:394
  6.0 0.1 tile.10
  6.1 0.6 %pad_add_fusion.lane_ref = s32[2,128]{1,0:T(2,128)} fusion(s32[1,128]{1,0:T(1,128)S(1)} %and_select_fusion.5, s32[1,128]{1,0:T(1,128)S(1)} %fusion.34), kind=kLoop, calls=%fused_computation.97 | loop fusion | flops 256 | bytes 2048 | tf_op jit(solution)/shard_map/stack | solution.py:396
  6.7 0.7 %fusion.45 = (s32[1,4,24]{2,1,0:T(4,128)S(1)}, s32[1,4,24]{2,1,0:T(4,128)S(1)}, f32[1,4,24]{2,1,0:T(4,128)S(1)}) fusion(s32[4,4,24]{2,1,0:T(4,128)} %param.11), kind=kLoop, calls=%fused_computation.135 | loop fusion | flops 96 | bytes 2304 | tf_op jit(solution)/shard_map/slice | solution.py:358
  7.4 0.1 reshape_squeeze.8
  7.5 0.1 reshape_squeeze.9
  7.6 0.7 %select_reduce_fusion.5 = s32[96]{0:T(128)S(1)} fusion(s32[16]{0:T(128)} %param.10, s32[96]{0:T(128)S(1)} %and_select_fusion.8), kind=kLoop, calls=%fused_computation.67 | loop fusion | flops 4512 | bytes 832 | tf_op jit(solution)/shard_map/reduce_sum | solution.py:340
  8.4 0.1 convert_element_type.57
  8.4 0.7 %select_reduce_fusion.4 = (f32[96]{0:T(128)S(1)}, f32[96]{0:T(128)S(1)}, f32[96]{0:T(128)S(1)}) fusion(f32[12]{0:T(128)S(1)} %get-tuple-element.55, s32[96]{0:T(128)S(1)} %reshape_squeeze.9, f32[12]{0:T(128)} %param.14, f32[12]{0:T(128)S(1)} %get-tuple-element.54), kind=kLoop, calls=%fused_computation.66 | loop fusion | flops 7776 | bytes 1680 | tf_op jit(solution)/shard_map/reduce_sum | solution.py:340
  9.2 0.2 convert_reduce_fusion.1
  9.4 0.1 reduce_sum.108
  9.5 1.4 %fusion.32 = (f32[4]{0:T(128)}, pred[1,4,24]{2,1,0:T(4,128)(4,1)S(1)}) fusion(f32[4,24]{1,0:T(4,128)S(1)} %reduce_sum.108, s32[4,4,24]{2,1,0:T(4,128)} %param.11), kind=kLoop, calls=%fused_computation.78 | loop fusion | flops 476 | bytes 1264 | tf_op jit(solution)/shard_map/reduce_sum | solution.py:370
  10.9 0.1 eq.387
  11.0 0.7 %copy.12.col_site_ref = s32[16,1]{1,0:T(8,128)} copy(s32[16,1]{0,1:T(1,128)S(1)} %pad_bitcast_fusion.1) | data formatting | bytes 128 | tf_op jit(solution)/shard_map/broadcast_in_dim | solution.py:503
  11.7 0.7 %copy.13.row_site_ref = s32[16,1]{1,0:T(8,128)} copy(s32[16,1]{0,1:T(1,128)S(1)} %pad_bitcast_fusion) | data formatting | bytes 128 | tf_op jit(solution)/shard_map/broadcast_in_dim | solution.py:504
  12.4 0.1 iota_compare_fusion.5
  12.5 0.1 iota_compare_fusion.3
  12.6 0.1 iota_compare_fusion.4
  12.6 0.9 %select_reduce_fusion.1 = (s32[16,128]{1,0:T(8,128)S(1)}, s32[16,128]{1,0:T(8,128)S(1)}, s32[16,128]{1,0:T(8,128)S(1)}) fusion(s32[96]{0:T(128)S(1)} %add_add_fusion.2, pred[128,96]{0,1:T(8,128)(4,1)S(1)} %iota_compare_fusion.4, pred[16,96]{1,0:T(8,128)(4,1)S(1)} %get-tuple-element.60, s32[96]{0:T(128)S(1)} %get-tuple-element.21, ...), kind=kLoop, calls=%fused_computation.23 | loop fusion | flops 1763328 | bytes 65664 | tf_op jit(solution)/shard_map/reduce_sum | solution.py:388
  13.6 0.6 %add_convert_fusion = f32[16,128]{1,0:T(8,128)} fusion(s32[16,128]{1,0:T(8,128)S(1)} %get-tuple-element.9, s32[16,128]{1,0:T(8,128)S(1)} %get-tuple-element.61, s32[16,128]{1,0:T(8,128)S(1)} %get-tuple-element.8), kind=kLoop, calls=%fused_computation.71 | loop fusion | flops 8192 | bytes 32768 | tf_op jit(solution)/shard_map/convert_element_type | solution.py:389
  14.1 0.1 iota_compare_fusion
  14.2 1.4 %pad_slice_fusion.7 = (f32[1,512]{1,0:T(1,128)S(1)}, f32[1,512]{1,0:T(1,128)S(1)}, f32[1,512]{1,0:T(1,128)S(1)}, f32[1,512]{1,0:T(1,128)S(1)}, f32[1,512]{1,0:T(...) fusion(f32[9,512]{1,0:T(8,128)} %param.15), kind=kLoop, calls=%fused_computation.50 | loop fusion | bytes 86016 | tf_op jit(solution)/shard_map/slice | solution.py:440
  15.6 0.1 select_select_fusion.2
  15.8 0.9 %fusion.21.mix_r_ref = f32[128,128]{1,0:T(8,128)} fusion(f32[128,96]{1,0:T(8,128)S(1)} %get-tuple-element.48, f32[128,96]{1,0:T(8,128)S(1)} %get-tuple-element.47, pred[96,128]{1,0:T(32,128)(4,1)S(1)} %get-tuple-element.62, pred[96,128]{1,0:T(32,128)(4,1)S(1)} %get-tuple-element.63), kind=kOutput, calls=%fused_computation.29 | convolution fusion | flops 37797888 | bytes 188416 | tf_op jit(solution)/shard_map/dot_general | solution.py:426
  16.6 0.9 %fusion.17 = f32[256,128]{1,0:T(8,128)} fusion(f32[128,96]{1,0:T(8,128)S(1)} %get-tuple-element.50, f32[128,96]{1,0:T(8,128)S(1)} %get-tuple-element.49, s32[96]{0:T(128)S(1)} %get-tuple-element.56), kind=kOutput, calls=%fused_computation.25 | convolution fusion | flops 37785600 | bytes 229760 | tf_op jit(solution)/shard_map/dot_general | solution.py:410
  17.6 1.5 %select_select_fusion = (f32[512,512]{1,0:T(8,128)S(1)}, f32[512,512]{1,0:T(8,128)}) fusion(f32[512]{0:T(512)S(1)} %bitcast.54, f32[512]{0:T(512)S(1)} %bitcast.55, f32[512]{0:T(512)S(1)} %bitcast.46, f32[512]{0:T(512)S(1)} %bitcast.47, f32[512]{0:T(512)S(1)} %bitcast.45, f32[512]{0:T(512)S(1)} %bitcast.48, f32[512]{0:T(512)S(1)} %bitcast.44, ...), kind=kLoop, calls=%fused_computation.2 | loop fusion | flops 9699328 | bytes 2131968 | tf_op jit(solution)/shard_map/jit(_where)/select_n | solution.py:439
  19.0 0.1 pad_dynamic-slice_fusion.1
  19.1 0.7 %dynamic_slice.13.loc_h_ref = f32[256,256]{1,0:T(8,128)} dynamic-slice(f32[512,512]{1,0:T(8,128)S(1)} %get-tuple-element.25, s32[]{:T(128)S(6)} %select_n.313, s32[]{:T(128)S(6)} %select_n.313), dynamic_slice_sizes={256,256} | dynamic-slice | bytes 524292 | tf_op jit(solution)/shard_map/dynamic_slice | solution.py:442
  19.8 0.7 %select_maximum_fusion.halo_h_ref = f32[16,16]{1,0:T(8,128)} fusion(f32[8,8]{1,0:T(8,128)S(1)} %get-tuple-element.24, f32[8,8]{1,0:T(8,128)S(1)} %get-tuple-element.23), kind=kLoop, calls=%fused_computation.62 | loop fusion | flops 1280 | bytes 1536 | tf_op jit(solution)/shard_map/concatenate | solution.py:449
  20.5 0.0 copy-done
  20.5 24.4 %exchange.1 = (f32[4,2,256,512]{3,2,1,0:T(8,128)}, f32[128,256]{1,0:T(8,128)}, f32[128,512]{1,0:T(8,128)}) custom-call(f32[16,1,128]{2,1,0:T(1,128)} %bitcast.38, s32[2,128]{1,0:T(2,128)} %pad_add_fusion.lane_ref, s32[6]{0:T(128)} %copy-done, f32[4]{0:T(128)} %get-tuple-element.19.damp_ref, f32[512,512]{1,0:T(8,128)} %get-tuple-element.26.neg_h_ref, ...), custom_call_target="tpu_custom_call" | custom-call | tf_op jit(solution)/shard_map/exchange/pallas_call | solution.py:459
  45.0 11.0 %finish.1 = (f32[4,2,256,512]{3,2,1,0:T(8,128)}, f32[4,2,256,512]{3,2,1,0:T(8,128)}) custom-call(f32[4]{0:T(128)} %compare_convert_fusion.live_ref, s32[16,1]{1,0:T(8,128)} %copy.12.col_site_ref, s32[16,1]{1,0:T(8,128)} %copy.13.row_site_ref, f32[128,256]{1,0:T(8,128)} %get-tuple-element.5.c_ref, f32[128,512]{1,0:T(8,128)} %get-tuple-element.6.r_ref, ...), custom_call_target="tpu_custom_call" | custom-call | tf_op jit(solution)/shard_map/finish/pallas_call | solution.py:508
  (15 shorter events, 0.1 us)
Async XLA Ops:
  1.4 19.2 %copy-start = (s32[6]{0:T(128)}, s32[6]{0:T(128)S(1)}, u32[]{:S(2)}) copy-start(s32[6]{0:T(128)S(1)} %dynamic-slice_subtract_fusion.site_ref) | copy-start | bytes 76

commit v2 on v1

v2 whole, which is shorter than its diff:
```python
import functools

import jax
import jax.numpy as jnp
from jax import lax
from jax.experimental import pallas as pl
from jax.experimental.pallas import tpu as pltpu
from jax.sharding import PartitionSpec as P

step_size = 0.05
MESH = pl.DeviceIdType.MESH
f32 = jnp.float32
bf16 = jnp.bfloat16


def up(value, unit):
    return (value + unit - 1) // unit * unit


def split(value):
    hi = value.astype(bf16)
    lo = (value - hi.astype(f32)).astype(bf16)
    return hi, lo


def mm(a, b):
    return lax.dot_general(a, b, (((1,), (0,)), ((), ())), preferred_element_type=f32)


def mm_nt(a, b):
    return lax.dot_general(a, b, (((1,), (1,)), ((), ())), preferred_element_type=f32)


def mm3(a, b):
    a_hi, a_lo = split(a)
    b_hi, b_lo = split(b)
    return mm(a_hi, b_hi) + (mm(a_hi, b_lo) + mm(a_lo, b_hi))


def banded(diff, bands, edge):
    total = jnp.where(diff == 0, bands[0:1, :], 0.0)
    for o in range(1, edge + 1):
        total = jnp.where(diff == o, bands[o : o + 1, :], total)
        total = jnp.where(diff == -o, pltpu.roll(bands, o, 1)[o : o + 1, :], total)
    return total


def exchange_kernel(
    dims,
    links_ref,
    counts_ref,
    site_ref,
    coef_ref,
    rate_ref,
    bands_ref,
    state_hbm,
    slope_hbm,
    d_buf,
    base_ref,
    c_ref,
    r_ref,
    spread_ref,
    row_at_ref,
    st,
    sl,
    z_hi,
    z_lo,
    h_hi,
    h_lo,
    bands_pad,
    req_ref,
    req_in,
    halo_st,
    halo_sl,
    col_acc,
    row_pack,
    sel_c,
    sel_r,
    send_c,
    send_r,
    recv_c,
    recv_r,
    load_sem,
    req_send,
    req_recv,
    halo_send,
    halo_recv,
    c_send,
    c_recv,
    r_send,
    r_recv,
):
    tiers, systems, slots, modes, block, edge, per_slot, rp, cw, rw = dims
    rows, levels = st.shape[1], st.shape[2]
    me = lax.axis_index("tier")
    sy = lax.axis_index("sys")
    planes = slots * 2

    def load(p):
        g, c = p // 2, p % 2
        return (
            pltpu.make_async_copy(state_hbm.at[g, c], st.at[p], load_sem.at[0, p]),
            pltpu.make_async_copy(slope_hbm.at[g, c], sl.at[p], load_sem.at[1, p]),
        )

    for p in range(planes):
        for copy in load(p):
            copy.start()

    barrier = pltpu.get_barrier_semaphore()

    def greet(i, carry):
        pl.semaphore_signal(
            barrier, inc=1, device_id=(lax.rem(me + i, tiers), sy), device_id_type=MESH
        )
        return carry

    lax.fori_loop(1, tiers, greet, 0)

    @pl.when(sy > 0)
    def _():
        pl.semaphore_signal(barrier, inc=1, device_id=(me, sy - 1), device_id_type=MESH)

    @pl.when(sy < systems - 1)
    def _():
        pl.semaphore_signal(barrier, inc=1, device_id=(me, sy + 1), device_id_type=MESH)

    total = slots * per_slot
    wide_q = up(total, 128)

    def iota(shape, axis):
        return lax.broadcasted_iota(jnp.int32, shape, axis).astype(f32)

    def flag(where):
        return jnp.where(where, 1.0, 0.0)

    flat = jnp.zeros((4, wide_q), f32)
    for g in range(slots):
        place = flag(
            iota((per_slot, wide_q), 1) == iota((per_slot, wide_q), 0) + float(g * per_slot)
        )
        flat += mm(links_ref[:, g, :].astype(f32).astype(bf16), place.astype(bf16))
    lane_q = iota((1, wide_q), 1)
    valid = lane_q < float(total)
    mode, kind, level = flat[1:2], flat[2:3], flat[3:4]
    holder = jnp.floor((flat[0:1] + 0.5) * (1.0 / slots))
    target = flat[0:1] - holder * float(slots)
    holder = jnp.where(valid, holder, -1.0)
    slot_of = jnp.where(valid, jnp.floor((lane_q + 0.5) * (1.0 / per_slot)), -1.0)
    first_mode = (sy * block).astype(f32)
    in_block = valid & (mode >= first_mode) & (mode < first_mode + float(block))
    local_mode = mode - first_mode
    has = flag(holder == iota((tiers, wide_q), 0))
    has_r = has * flag(in_block)
    before = flag(iota((wide_q, wide_q), 0) < iota((wide_q, wide_q), 1)).astype(bf16)
    rank_c = jnp.sum(has * mm(has.astype(bf16), before), axis=0, keepdims=True)
    rank_r = jnp.sum(has_r * mm(has_r.astype(bf16), before), axis=0, keepdims=True)
    lane_j = iota((128, wide_q), 0)

    def asked(codes, ranks):
        return mm_nt(codes.astype(bf16), flag(lane_j == ranks).astype(bf16))

    req = asked(has * (target * float(modes) + mode + 1.0), rank_c) - 1.0
    for c in range(2):
        code = (target + float(c * slots)) * float(block) + local_mode + 1.0
        req += asked(has_r * code, rank_r + float(cw + c * rp))
    for t in range(tiers):
        req_ref[t] = req[t : t + 1, :]

    inner = (sy > 0).astype(jnp.int32) + (sy < systems - 1).astype(jnp.int32)
    pl.semaphore_wait(barrier, tiers - 1 + inner)

    def send(src, dst, send_sem, recv_sem, i):
        peer = lax.rem(me + i, tiers)
        return pltpu.make_async_remote_copy(
            src_ref=src.at[peer],
            dst_ref=dst.at[me],
            send_sem=send_sem.at[i],
            recv_sem=recv_sem.at[i],
            device_id=(peer, sy),
            device_id_type=MESH,
        )

    def receive(src, dst, send_sem, recv_sem, i):
        peer = lax.rem(me + tiers - i, tiers)
        return pltpu.make_async_remote_copy(
            src_ref=src.at[peer],
            dst_ref=dst.at[peer],
            send_sem=send_sem.at[i],
            recv_sem=recv_sem.at[i],
            device_id=(peer, sy),
            device_id_type=MESH,
        )

    def req_start(i, carry):
        send(req_ref, req_in, req_send, req_recv, i).start()
        return carry

    lax.fori_loop(1, tiers, req_start, 0)

    def halo(side):
        first = rows - edge if side == 0 else 0
        target = sy + 1 if side == 0 else sy - 1
        return [
            pltpu.make_async_remote_copy(
                src_ref=src.at[:, :, pl.ds(first, edge), :],
                dst_ref=dst.at[side],
                send_sem=halo_send.at[side, n],
                recv_sem=halo_recv.at[side, n],
                device_id=(me, target),
                device_id_type=MESH,
            )
            for n, (src, dst) in enumerate(((state_hbm, halo_st), (slope_hbm, halo_sl)))
        ]

    @pl.when(sy < systems - 1)
    def _():
        for copy in halo(0):
            copy.start()

    @pl.when(sy > 0)
    def _():
        for copy in halo(1):
            copy.start()

    @pl.when(sy == 0)
    def _():
        halo_st[0] = jnp.zeros_like(halo_st[0])
        halo_sl[0] = jnp.zeros_like(halo_sl[0])

    @pl.when(sy == systems - 1)
    def _():
        halo_st[1] = jnp.zeros_like(halo_st[1])
        halo_sl[1] = jnp.zeros_like(halo_sl[1])

    req_in[me] = req_ref[me]
    row_pack[...] = jnp.zeros_like(row_pack)
    width = col_acc.shape[-1]
    lane_gm = iota((1, width), 1)
    lane_slot = jnp.floor((lane_gm + 0.5) * (1.0 / modes))
    lane_mode = lane_gm - lane_slot * float(modes)
    lane_site = jnp.zeros((1, width), jnp.int32)
    for k in range(modes):
        lane_site = jnp.where(lane_mode == float(k), site_ref[k], lane_site)
    level_at = lax.broadcasted_iota(jnp.int32, (levels, width), 0)
    for g in range(slots):
        pick = jnp.where((level_at == lane_site) & (lane_slot == float(g)), 1.0, 0.0).astype(bf16)
        for c in range(2):
            p = g * 2 + c
            for copy in load(p):
                copy.wait()
            hi, lo = split(st[p] + (0.5 * step_size) * sl[p])
            z_hi[p] = hi
            z_lo[p] = lo
            col_hi = mm(hi, pick)
            col_lo = mm(lo, pick)
            if g == 0:
                col_acc[c] = col_hi
                col_acc[2 + c] = col_lo
            else:
                col_acc[c] += col_hi
                col_acc[2 + c] += col_lo
    for c in range(2):
        for g in range(slots):
            for k in range(block):
                at = jnp.clip(site_ref[sy * block + k] - sy * rows, 0, rows - 1)
                p = g * 2 + c
                row = st[p, pl.ds(at, 1), :] + (0.5 * step_size) * sl[p, pl.ds(at, 1), :]
                dest = (c * slots + g) * block + k
                row_pack[dest : dest + 1, :] = row

    row_start = sy * rows
    bands_pad[...] = jnp.zeros_like(bands_pad)
    bands_pad[0 : edge + 1, :] = bands_ref[...]
    bands = bands_pad[...]
    strip = min(128, levels)

    def dense(i, carry):
        at = pl.multiple_of(i * strip, strip)
        diff = (
            lax.broadcasted_iota(jnp.int32, (strip, levels), 0)
            + at
            - lax.broadcasted_iota(jnp.int32, (strip, levels), 1)
        )
        hi, lo = split(-banded(diff, bands, edge))
        h_hi[pl.ds(at, strip), :] = hi
        h_lo[pl.ds(at, strip), :] = lo
        return carry

    lax.fori_loop(0, levels // strip, dense, 0)

    def rolled(shift):
        return pltpu.roll(bands, lax.rem(shift + 2 * levels, levels), 1)

    wide_r = up(rows, 128)
    diff = lax.broadcasted_iota(jnp.int32, (rows, wide_r), 0) - lax.broadcasted_iota(
        jnp.int32, (rows, wide_r), 1
    )
    near_bands = rolled(-row_start)
    loc = jnp.where(diff == 0, near_bands[0:1, :wide_r], 0.0)
    for o in range(1, edge + 1):
        loc = jnp.where(diff == o, near_bands[o : o + 1, :wide_r], loc)
        loc = jnp.where(diff == -o, pltpu.roll(near_bands, o, 1)[o : o + 1, :wide_r], loc)
    loc_hi, loc_lo = split(loc[:, :rows])
    sub = lax.broadcasted_iota(jnp.int32, (2 * edge, 128), 0)
    lan = lax.broadcasted_iota(jnp.int32, (2 * edge, 128), 1)
    low_bands = rolled(edge - row_start)
    high_bands = rolled(edge - row_start - rows)
    halo_h = jnp.zeros((2 * edge, 128), f32)
    for o in range(edge + 1):
        low = (sub < edge) & (lan < edge) & (edge + sub - lan == o)
        high = (sub >= edge) & (lan >= edge) & (lan < 2 * edge) & (edge + lan - sub == o)
        above = pltpu.roll(high_bands, o, 1) if o else high_bands
        halo_h = jnp.where(low, low_bands[o : o + 1, :128], halo_h)
        halo_h = jnp.where(high, above[o : o + 1, :128], halo_h)
    halo_h = halo_h[:, : 2 * edge]

    def req_wait(i, carry):
        receive(req_ref, req_in, req_send, req_recv, i).wait_recv()
        return carry

    lax.fori_loop(1, tiers, req_wait, 0)
    codes = jnp.transpose(req_in[:, 0, :])
    lane_c = lax.broadcasted_iota(jnp.int32, (cw, sel_c.shape[1]), 1).astype(f32)
    lane_r = lax.broadcasted_iota(jnp.int32, (rw, sel_r.shape[1]), 1).astype(f32)
    for t in range(tiers):
        sel_c[t * cw : (t + 1) * cw, :] = jnp.where(codes[0:cw, t : t + 1] == lane_c, 1.0, 0.0)
        sel_r[t * rw : (t + 1) * rw, :] = jnp.where(
            codes[cw : cw + rw, t : t + 1] == lane_r, 1.0, 0.0
        )
    pick_c = sel_c[...].astype(bf16)
    pick_r = sel_r[...].astype(bf16)
    pack_hi, pack_lo = split(row_pack[...])
    send_r[...] = (mm(pick_r, pack_hi) + mm(pick_r, pack_lo)).reshape(tiers, rw, levels)
    for c in range(2):
        packed = mm_nt(pick_c, col_acc[c].astype(bf16)) + mm_nt(
            pick_c, col_acc[2 + c].astype(bf16)
        )
        send_c[:, :, c * rows : (c + 1) * rows] = packed.reshape(tiers, cw, rows)

    def pack_start(i, carry):
        send(send_r, recv_r, r_send, r_recv, i).start()
        send(send_c, recv_c, c_send, c_recv, i).start()
        return carry

    lax.fori_loop(1, tiers, pack_start, 0)
    recv_c[me] = send_c[me]
    recv_r[me] = send_r[me]

    @pl.when(sy > 0)
    def _():
        for copy in halo(0):
            copy.wait_recv()

    @pl.when(sy < systems - 1)
    def _():
        for copy in halo(1):
            copy.wait_recv()

    def table(ref, count, index):
        value = jnp.zeros((1, wide_q), f32)
        for k in range(count):
            value = jnp.where(index == float(k), ref(k), value)
        return value

    own_count = counts_ref[me].astype(f32)
    near = flag(target < table(lambda k: counts_ref[k].astype(f32), tiers, holder))
    near = near * flag(slot_of < own_count)
    down = kind == 1.0
    w_re = jnp.where(down, level * table(lambda k: coef_ref[0, k], modes, mode), 1.0) * near
    w_im = jnp.where(down, level * table(lambda k: coef_ref[1, k], modes, mode), 0.0) * near
    rate = jnp.where(down, level * table(lambda k: rate_ref[k], modes, mode), 0.0)
    wide_m, wide_b = spread_ref.shape[0], row_at_ref.shape[0]

    def mixing(wide, index, mask, signs):
        from_re, from_im = [], []
        for g in range(slots):
            own = flag((iota((wide, wide_q), 0) == index) & (slot_of == float(g)) & mask)
            for re, im in signs:
                from_re.append(own * re)
                from_im.append(own * im)
        return jnp.concatenate(from_re, axis=0), jnp.concatenate(from_im, axis=0)

    def packets(count, at, mask):
        return flag((iota((count, wide_q), 0) == at) & mask).astype(bf16)

    def place(value, at):
        hi, lo = split(value)
        return mm_nt(hi, at) + mm_nt(lo, at)

    at_c = packets(tiers * cw, holder * float(cw) + rank_c, valid)
    from_re, from_im = mixing(wide_m, mode, valid, ((w_im, -w_re), (w_re, w_im)))
    mix_c = (place(from_re, at_c), place(from_im, at_c))
    from_re, from_im = mixing(wide_b, local_mode, in_block, ((w_im, w_re), (-w_re, w_im)))
    at_row = holder * float(rw) + rank_r
    mix_r = place(from_re, packets(tiers * rw, at_row, in_block)) + place(
        from_im, packets(tiers * rw, at_row + float(rp), in_block)
    )
    site_lane = lax.broadcasted_iota(jnp.int32, (1, levels), 1)
    spread_ref[...] = jnp.zeros_like(spread_ref)
    for k in range(modes):
        spread_ref[k : k + 1, :] = flag(site_lane == site_ref[k])
    row_lane = lax.broadcasted_iota(jnp.int32, (1, rows), 1)
    row_at_ref[...] = jnp.zeros_like(row_at_ref)
    for k in range(block):
        row_at_ref[k : k + 1, :] = flag(row_lane == site_ref[sy * block + k] - row_start)

    def commute(p):
        hi, lo = z_hi[p], z_lo[p]
        g, c = p // 2, p % 2
        neg_hi = h_hi[...]
        both = mm(loc_hi, hi) + mm(hi, neg_hi)
        both += mm(loc_hi, lo) + mm(hi, h_lo[...])
        both += mm(loc_lo, hi) + mm(lo, neg_hi)
        ghost = [halo_st[s, g, c] + (0.5 * step_size) * halo_sl[s, g, c] for s in range(2)]
        extra = mm3(halo_h, jnp.concatenate(ghost, axis=0))
        return both, extra

    for g in range(slots):
        live = flag(own_count > float(g))
        damp = jnp.sum(jnp.where(slot_of == float(g), rate, 0.0), axis=1, keepdims=True) * live
        for c in range(2):
            both, extra = commute(g * 2 + 1 - c)
            p = g * 2 + c
            sign = live if c == 0 else -live
            mid = st[p] + (0.5 * step_size) * sl[p]
            d_buf[p] = sign * both - damp * mid
            d_buf[p, 0:edge, :] += sign * extra[0:edge]
            d_buf[p, rows - edge : rows, :] += sign * extra[edge : 2 * edge]
            base_ref[p] = live * (st[p] + (step_size / 6.0) * sl[p])

    def pack_wait(i, carry):
        receive(send_r, recv_r, r_send, r_recv, i).wait_recv()
        receive(send_c, recv_c, c_send, c_recv, i).wait_recv()
        return carry

    lax.fori_loop(1, tiers, pack_wait, 0)
    got_c = recv_c[...].reshape(tiers * cw, 2 * rows)
    got_r = recv_r[...].reshape(tiers * rw, levels)
    r_ref[...] = mm3(mix_r, got_r)
    c_ref[...] = mm3(mix_c[0], got_c[:, 0:rows]) + mm3(mix_c[1], got_c[:, rows : 2 * rows])

    def finish(i, carry):
        send(req_ref, req_in, req_send, req_recv, i).wait_send()
        send(send_r, recv_r, r_send, r_recv, i).wait_send()
        send(send_c, recv_c, c_send, c_recv, i).wait_send()
        return carry

    lax.fori_loop(1, tiers, finish, 0)

    @pl.when(sy < systems - 1)
    def _():
        for copy in halo(0):
            copy.wait_send()

    @pl.when(sy > 0)
    def _():
        for copy in halo(1):
            copy.wait_send()


def finish_kernel(spread_ref, row_at_ref, c_ref, r_ref, d_ref, base_ref, next_ref, sum_ref):
    p = pl.program_id(0)
    spread = spread_ref[...].astype(bf16)
    row_at = row_at_ref[...]
    wide_m, wide_b = spread_ref.shape[0], row_at_ref.shape[0]
    col = c_ref[pl.ds(pl.multiple_of(p * wide_m, wide_m), wide_m), :]
    col_hi = col.astype(bf16).astype(f32)
    left = jnp.concatenate([col_hi, col - col_hi, row_at, row_at], axis=0)
    row_hi, row_lo = split(r_ref[pl.ds(pl.multiple_of(p * wide_b, wide_b), wide_b), :])
    right = jnp.concatenate([spread, spread, row_hi, row_lo], axis=0)
    slope_next = d_ref[p] + mm(jnp.transpose(left).astype(bf16), right)
    next_ref[0] = slope_next
    sum_ref[0] = base_ref[p] + step_size / 3.0 * slope_next


def shards(tiers, systems, state, slope, counts, links, mode_site, mode_coef, mode_rate, h_bands):
    slots, _, rows, levels = state.shape
    edge = h_bands.shape[0] - 1
    modes = mode_site.shape[0]
    block = modes // systems
    per_slot = links.shape[2]
    total = slots * per_slot
    cp = total // tiers
    rp = 2 * -(-(slots * block) // tiers)
    cw, rw = up(cp, 8), up(2 * rp, 8)
    wide_m, wide_b = up(modes, 16), up(block, 16)
    vmem = pl.BlockSpec(memory_space=pltpu.VMEM)
    smem = pl.BlockSpec(memory_space=pltpu.SMEM)
    hbm = pl.BlockSpec(memory_space=pl.ANY)
    planes = slots * 2
    wide_gm = up(slots * modes, 128)
    wide_rp = up(2 * slots * block, 128)
    dma = pltpu.SemaphoreType.DMA
    big = (planes, rows, levels)
    deriv, base, col_mix, row_mix, spread, row_at = pl.pallas_call(
        functools.partial(
            exchange_kernel, (tiers, systems, slots, modes, block, edge, per_slot, rp, cw, rw)
        ),
        out_shape=(
            pltpu.VMEM(big, f32),
            pltpu.VMEM(big, f32),
            pltpu.VMEM((planes * wide_m, rows), f32),
            pltpu.VMEM((planes * wide_b, levels), f32),
            pltpu.VMEM((wide_m, levels), f32),
            pltpu.VMEM((wide_b, rows), f32),
        ),
        in_specs=[vmem, smem, smem, smem, smem, vmem, hbm, hbm],
        out_specs=(vmem,) * 6,
        scratch_shapes=[
            pltpu.VMEM((planes, rows, levels), f32),
            pltpu.VMEM((planes, rows, levels), f32),
            pltpu.VMEM((planes, rows, levels), bf16),
            pltpu.VMEM((planes, rows, levels), bf16),
            pltpu.VMEM((levels, levels), bf16),
            pltpu.VMEM((levels, levels), bf16),
            pltpu.VMEM((up(edge + 1, 8), levels), f32),
            pltpu.VMEM((tiers, 1, 128), f32),
            pltpu.VMEM((tiers, 1, 128), f32),
            pltpu.VMEM((2, slots, 2, edge, levels), f32),
            pltpu.VMEM((2, slots, 2, edge, levels), f32),
            pltpu.VMEM((4, rows, wide_gm), f32),
            pltpu.VMEM((wide_rp, levels), f32),
            pltpu.VMEM((tiers * cw, wide_gm), f32),
            pltpu.VMEM((tiers * rw, wide_rp), f32),
            pltpu.VMEM((tiers, cw, 2 * rows), f32),
            pltpu.VMEM((tiers, rw, levels), f32),
            pltpu.VMEM((tiers, cw, 2 * rows), f32),
            pltpu.VMEM((tiers, rw, levels), f32),
            dma((2, planes)),
            dma((tiers,)),
            dma((tiers,)),
            dma((2, 2)),
            dma((2, 2)),
            dma((tiers,)),
            dma((tiers,)),
            dma((tiers,)),
            dma((tiers,)),
        ],
        compiler_params=pltpu.CompilerParams(
            collective_id=0, has_side_effects=True, vmem_limit_bytes=32 << 20
        ),
        name="exchange",
    )(links, counts, mode_site, mode_coef, mode_rate, h_bands, state, slope)
    plane = pl.BlockSpec((1, rows, levels), lambda p: (p, 0, 0))
    outs = pl.pallas_call(
        finish_kernel,
        grid=(planes,),
        out_shape=(jax.ShapeDtypeStruct(big, f32),) * 2,
        in_specs=[vmem] * 6,
        out_specs=(plane, plane),
        compiler_params=pltpu.CompilerParams(vmem_limit_bytes=16 << 20),
        name="finish",
    )(spread, row_at, col_mix, row_mix, deriv, base)
    return tuple(out.reshape(state.shape) for out in outs)


def solution(mesh):
    in_specs = (
        P("tier", None, "sys", None),
        P("tier", None, "sys", None),
        P(),
        P(None, "tier", None),
        P(),
        P(),
        P(),
        P(),
    )
    out_specs = (P("tier", None, "sys", None), P("tier", None, "sys", None))
    body = functools.partial(shards, mesh.shape["tier"], mesh.shape["sys"])
    return jax.shard_map(body, mesh=mesh, in_specs=in_specs, out_specs=out_specs, check_vma=False)
```

time: 56.6 us -> 39.3 us (0.69)
  other arithmetic: 11.9 us -> 0 us
  Pallas kernels: 35.4 us -> 29.9 us
  local copies, waits for them, and re-layouts: 6.11 us -> 8.46 us
  matrix products: 1.81 us -> 0 us
    unnamed x2 -> x16, local copies, waits for them, and re-layouts: 0.01 us -> 8.46 us
    pallas_call x1, Pallas kernels: 11 us -> 5.3 us  [shards(): pl.pallas_call(finish_kernel, grid=(planes,), out_shape=(jax.ShapeDtypeSt...]
    reduce_sum x6 -> x0, other arithmetic: 5.25 us -> none  [the longest x3 2.78 us: lookup(): jnp.sum(jnp.where(matches, table, jnp.zeros((), table.dtype)), axis=-1)]
    broadcast_in_dim x4 -> x0, local copies, waits for them, and re-layouts: 2.01 us -> none  [the longest x2 1.34 us: shards(): jnp.pad(mode_site, (0, wide_m - modes), constant_values=-1)[:, None]]
    convert_element_type x2 -> x0, other arithmetic: 1.83 us -> none  [the longest x1 1.24 us: shards(): (jnp.arange(slots, dtype=jnp.int32) < lookup(tier_index, counts)).astype(...]
    dot_general x2 -> x0, matrix products: 1.81 us -> none  [the longest x1 0.92 us: shards(): jnp.dot(jnp.concatenate([coef_from_re, coef_from_im]), at_c, precision=hp)]
    select_n x6 -> x0, other arithmetic: 1.62 us -> none  [the longest x1 1.47 us: shards(): jnp.where(j_at - i_at == o, shifted[o, edge - o:edge - o + levels][None,...]
    slice x1 -> x0, local copies, waits for them, and re-layouts: 1.37 us -> none  [shards(): shifted[o, edge - o:edge - o + levels][None, :]]
where the time goes in v2:
time: 39.3 us; the launch traced here: 39 us
  Pallas kernels  29.9 us (76%)
  local copies, waits for them, and re-layouts  8.46 us (22%)
  between operations  0.66 us (2%)
    pallas_call x1, Pallas kernels, shards(): pl.pallas_call(functools.partial(exchange_kernel, (tiers, systems, slots,...  24.6 us
    unnamed x16, local copies, waits for them, and re-layouts  8.46 us
    pallas_call x1, Pallas kernels, shards(): pl.pallas_call(finish_kernel, grid=(planes,), out_shape=(jax.ShapeDtypeSt...  5.3 us

profile of v2, /device:TPU:11, one launch (start us, length us, event | category | flops | bytes accessed | tf_op | source)
XLA Modules:
  0.0 39.0 jit_solution(411829623567804264)
XLA Ops:
  0.6 0.0 copy-start
  0.6 2.2 %copy-done = f32[4,2,256,512]{3,2,1,0:T(8,128)S(1)} copy-done((f32[4,2,256,512]{3,2,1,0:T(8,128)S(1)}, f32[4,2,256,512]{3,2,1,0:T(8,128)}, u32[]{:S(2)}) %copy-start) | copy-done | bytes 4194328
  2.8 0.0 copy-start.1
  2.8 2.2 %copy-done.1 = f32[4,2,256,512]{3,2,1,0:T(8,128)S(1)} copy-done((f32[4,2,256,512]{3,2,1,0:T(8,128)S(1)}, f32[4,2,256,512]{3,2,1,0:T(8,128)}, u32[]{:S(2)}) %copy-start.1) | copy-done | bytes 4194328
  5.0 0.0 copy-start.2
  5.0 0.8 %copy-done.2 = f32[9,512]{1,0:T(8,128)S(1)} copy-done((f32[9,512]{1,0:T(8,128)S(1)}, f32[9,512]{1,0:T(8,128)}, u32[]{:S(2)}) %copy-start.2) | copy-done | bytes 18456
  5.8 0.0 copy-start.3
  5.8 0.7 %copy-done.3 = s32[4,4,24]{2,1,0:T(4,128)S(1)} copy-done((s32[4,4,24]{2,1,0:T(4,128)S(1)}, s32[4,4,24]{2,1,0:T(4,128)}, u32[]{:S(2)}) %copy-start.3) | copy-done | bytes 1560
  6.5 0.0 copy-start.4
  6.5 0.7 %copy-done.4 = f32[2,12]{1,0:T(2,128)S(1)} copy-done((f32[2,12]{1,0:T(2,128)S(1)}, f32[2,12]{1,0:T(2,128)}, u32[]{:S(2)}) %copy-start.4) | copy-done | bytes 120
  7.1 0.0 copy-start.5
  7.1 0.7 %copy-done.5 = s32[16]{0:T(128)S(1)} copy-done((s32[16]{0:T(128)S(1)}, s32[16]{0:T(128)}, u32[]{:S(2)}) %copy-start.5) | copy-done | bytes 88
  7.8 0.0 copy-start.6
  7.8 0.7 %copy-done.6 = s32[12]{0:T(128)S(1)} copy-done((s32[12]{0:T(128)S(1)}, s32[12]{0:T(128)}, u32[]{:S(2)}) %copy-start.6) | copy-done | bytes 72
  8.5 0.0 copy-start.7
  8.5 0.7 %copy-done.7 = f32[12]{0:T(128)S(1)} copy-done((f32[12]{0:T(128)S(1)}, f32[12]{0:T(128)}, u32[]{:S(2)}) %copy-start.7) | copy-done | bytes 72
  9.1 24.6 %exchange.1 = (f32[8,256,512]{2,1,0:T(8,128)S(1)}, f32[8,256,512]{2,1,0:T(8,128)S(1)}, f32[128,256]{1,0:T(8,128)S(1)}, f32[128,512]{1,0:T(8,128)S(1)}, f32[16,512]{1,0:T(8,128)S(1)}, /*index=5*/f32[16,256]{1,0:T(8,128)S(1)}) custom-call(s32[4,4,24]{2,1,0:T(4,128)S(1)} %copy-done.3, s32[16]{0:T(128)S(1)} %copy-done.5, s32[12]{0:T(128)S(1)} %copy-done.6, ...), custom_call_target="tpu_custom_call" | custom-call | tf_op jit(solution)/shard_map/exchange/pallas_call | solution.py:496
  33.7 5.3 %finish.1 = (f32[8,256,512]{2,1,0:T(8,128)}, f32[8,256,512]{2,1,0:T(8,128)}) custom-call(f32[16,512]{1,0:T(8,128)S(1)} %get-tuple-element.10.spread_ref, f32[16,256]{1,0:T(8,128)S(1)} %get-tuple-element.11.row_at_ref, f32[128,256]{1,0:T(8,128)S(1)} %get-tuple-element.12.c_ref, f32[128,512]{1,0:T(8,128)S(1)} %get-tuple-element.13.r_ref, ...), custom_call_target="tpu_custom_call" | custom-call | tf_op jit(solution)/shard_map/finish/pallas_call | solution.py:546
Async XLA Ops:
  0.6 2.2 %copy-start = (f32[4,2,256,512]{3,2,1,0:T(8,128)S(1)}, f32[4,2,256,512]{3,2,1,0:T(8,128)}, u32[]{:S(2)}) copy-start(f32[4,2,256,512]{3,2,1,0:T(8,128)} %state_hbm.1) | copy-start | bytes 12582916
  2.8 2.2 %copy-start.1 = (f32[4,2,256,512]{3,2,1,0:T(8,128)S(1)}, f32[4,2,256,512]{3,2,1,0:T(8,128)}, u32[]{:S(2)}) copy-start(f32[4,2,256,512]{3,2,1,0:T(8,128)} %slope_hbm.1) | copy-start | bytes 12582916
  5.0 0.8 %copy-start.2 = (f32[9,512]{1,0:T(8,128)S(1)}, f32[9,512]{1,0:T(8,128)}, u32[]{:S(2)}) copy-start(f32[9,512]{1,0:T(8,128)} %bands_ref.1) | copy-start | bytes 55300
  5.8 0.7 %copy-start.3 = (s32[4,4,24]{2,1,0:T(4,128)S(1)}, s32[4,4,24]{2,1,0:T(4,128)}, u32[]{:S(2)}) copy-start(s32[4,4,24]{2,1,0:T(4,128)} %links_ref.1) | copy-start | bytes 4612
  6.5 0.7 %copy-start.4 = (f32[2,12]{1,0:T(2,128)S(1)}, f32[2,12]{1,0:T(2,128)}, u32[]{:S(2)}) copy-start(f32[2,12]{1,0:T(2,128)} %coef_ref.1) | copy-start | bytes 292
  7.1 0.7 %copy-start.5 = (s32[16]{0:T(128)S(1)}, s32[16]{0:T(128)}, u32[]{:S(2)}) copy-start(s32[16]{0:T(128)} %counts_ref.1) | copy-start | bytes 196
  7.8 0.7 %copy-start.6 = (s32[12]{0:T(128)S(1)}, s32[12]{0:T(128)}, u32[]{:S(2)}) copy-start(s32[12]{0:T(128)} %site_ref.1) | copy-start | bytes 148
  8.5 0.7 %copy-start.7 = (f32[12]{0:T(128)S(1)}, f32[12]{0:T(128)}, u32[]{:S(2)}) copy-start(f32[12]{0:T(128)} %rate_ref.1) | copy-start | bytes 148

commit v3 on v2

--- a/solution.py
+++ b/solution.py
@@ -47,12 +47,12 @@
 
 def exchange_kernel(
     dims,
-    links_ref,
-    counts_ref,
-    site_ref,
-    coef_ref,
-    rate_ref,
-    bands_ref,
+    links_hbm,
+    counts_hbm,
+    site_hbm,
+    coef_hbm,
+    rate_hbm,
+    bands_hbm,
     state_hbm,
     slope_hbm,
     d_buf,
@@ -61,6 +61,12 @@
     r_ref,
     spread_ref,
     row_at_ref,
+    links_ref,
+    counts_ref,
+    site_ref,
+    coef_ref,
+    rate_ref,
+    bands_ref,
     st,
     sl,
     z_hi,
@@ -89,6 +95,7 @@
     c_recv,
     r_send,
     r_recv,
+    small_sem,
 ):
     tiers, systems, slots, modes, block, edge, per_slot, rp, cw, rw = dims
     rows, levels = st.shape[1], st.shape[2]
@@ -103,6 +110,21 @@
             pltpu.make_async_copy(slope_hbm.at[g, c], sl.at[p], load_sem.at[1, p]),
         )
 
+    small = [
+        pltpu.make_async_copy(src, dst, small_sem.at[n])
+        for n, (src, dst) in enumerate(
+            (
+                (links_hbm, links_ref),
+                (counts_hbm, counts_ref),
+                (site_hbm, site_ref),
+                (coef_hbm, coef_ref),
+                (rate_hbm, rate_ref),
+                (bands_hbm, bands_ref),
+            )
+        )
+    ]
+    for copy in small:
+        copy.start()
     for p in range(planes):
         for copy in load(p):
             copy.start()
@@ -134,6 +156,8 @@
     def flag(where):
         return jnp.where(where, 1.0, 0.0)
 
+    for copy in small:
+        copy.wait()
     flat = jnp.zeros((4, wide_q), f32)
     for g in range(slots):
         place = flag(
@@ -485,9 +509,9 @@
     rp = 2 * -(-(slots * block) // tiers)
     cw, rw = up(cp, 8), up(2 * rp, 8)
     wide_m, wide_b = up(modes, 16), up(block, 16)
+    arrays = (links, counts, mode_site, mode_coef, mode_rate, h_bands, state, slope)
     vmem = pl.BlockSpec(memory_space=pltpu.VMEM)
-    smem = pl.BlockSpec(memory_space=pltpu.SMEM)
-    hbm = pl.BlockSpec(memory_space=pl.ANY)
+    hbm = pl.BlockSpec(memory_space=pltpu.HBM)
     planes = slots * 2
     wide_gm = up(slots * modes, 128)
     wide_rp = up(2 * slots * block, 128)
@@ -505,9 +529,15 @@
             pltpu.VMEM((wide_m, levels), f32),
             pltpu.VMEM((wide_b, rows), f32),
         ),
-        in_specs=[vmem, smem, smem, smem, smem, vmem, hbm, hbm],
+        in_specs=[hbm] * 8,
         out_specs=(vmem,) * 6,
         scratch_shapes=[
+            pltpu.VMEM(links.shape, jnp.int32),
+            pltpu.SMEM(counts.shape, jnp.int32),
+            pltpu.SMEM(mode_site.shape, jnp.int32),
+            pltpu.SMEM(mode_coef.shape, f32),
+            pltpu.SMEM(mode_rate.shape, f32),
+            pltpu.VMEM(h_bands.shape, f32),
             pltpu.VMEM((planes, rows, levels), f32),
             pltpu.VMEM((planes, rows, levels), f32),
             pltpu.VMEM((planes, rows, levels), bf16),
@@ -536,12 +566,13 @@
             dma((tiers,)),
             dma((tiers,)),
             dma((tiers,)),
+            dma((6,)),
         ],
         compiler_params=pltpu.CompilerParams(
             collective_id=0, has_side_effects=True, vmem_limit_bytes=32 << 20
         ),
         name="exchange",
-    )(links, counts, mode_site, mode_coef, mode_rate, h_bands, state, slope)
+    )(*(pltpu.with_memory_space_constraint(x, pltpu.HBM) for x in arrays))
     plane = pl.BlockSpec((1, rows, levels), lambda p: (p, 0, 0))
     outs = pl.pallas_call(
         finish_kernel,

time: 39.3 us -> 30.6 us (0.78)
  local copies, waits for them, and re-layouts: 8.46 us -> 0 us
    unnamed x16 -> x0, local copies, waits for them, and re-layouts: 8.46 us -> none
where the time goes in v3:
time: 30.6 us; the launch traced here: 30.3 us
  Pallas kernels  29.6 us (97%)
  between operations  0.64 us (2%)
    pallas_call x1, Pallas kernels, shards(): pl.pallas_call(functools.partial(exchange_kernel, (tiers, systems, slots,...  24.3 us
    pallas_call x1, Pallas kernels, shards(): pl.pallas_call(finish_kernel, grid=(planes,), out_shape=(jax.ShapeDtypeSt...  5.3 us

profile of v3, /device:TPU:11, one launch (start us, length us, event | category | flops | bytes accessed | tf_op | source)
XLA Modules:
  0.0 30.3 jit_solution(11235139265598625197)
XLA Ops:
  0.6 24.3 %exchange.1 = (f32[8,256,512]{2,1,0:T(8,128)S(1)}, f32[8,256,512]{2,1,0:T(8,128)S(1)}, f32[128,256]{1,0:T(8,128)S(1)}, f32[128,512]{1,0:T(8,128)S(1)}, f32[16,512]{1,0:T(8,128)S(1)}, /*index=5*/f32[16,256]{1,0:T(8,128)S(1)}) custom-call(s32[4,4,24]{2,1,0:T(4,128)} %links_hbm.1, s32[16]{0:T(128)} %counts_hbm.1, s32[12]{0:T(128)} %site_hbm.1, ...), custom_call_target="tpu_custom_call" | custom-call | tf_op jit(solution)/shard_map/exchange/pallas_call | solution.py:520
  25.0 5.3 %finish.1 = (f32[8,256,512]{2,1,0:T(8,128)}, f32[8,256,512]{2,1,0:T(8,128)}) custom-call(f32[16,512]{1,0:T(8,128)S(1)} %get-tuple-element.10.spread_ref, f32[16,256]{1,0:T(8,128)S(1)} %get-tuple-element.11.row_at_ref, f32[128,256]{1,0:T(8,128)S(1)} %get-tuple-element.12.c_ref, f32[128,512]{1,0:T(8,128)S(1)} %get-tuple-element.13.r_ref, ...), custom_call_target="tpu_custom_call" | custom-call | tf_op jit(solution)/shard_map/finish/pallas_call | solution.py:577

commit v4 on v3

--- a/solution.py
+++ b/solution.py
@@ -293,6 +293,38 @@
                 dest = (c * slots + g) * block + k
                 row_pack[dest : dest + 1, :] = row
 
+    def req_wait(i, carry):
+        receive(req_ref, req_in, req_send, req_recv, i).wait_recv()
+        return carry
+
+    lax.fori_loop(1, tiers, req_wait, 0)
+    codes = jnp.transpose(req_in[:, 0, :])
+    lane_c = lax.broadcasted_iota(jnp.int32, (cw, sel_c.shape[1]), 1).astype(f32)
+    lane_r = lax.broadcasted_iota(jnp.int32, (rw, sel_r.shape[1]), 1).astype(f32)
+    for t in range(tiers):
+        sel_c[t * cw : (t + 1) * cw, :] = jnp.where(codes[0:cw, t : t + 1] == lane_c, 1.0, 0.0)
+        sel_r[t * rw : (t + 1) * rw, :] = jnp.where(
+            codes[cw : cw + rw, t : t + 1] == lane_r, 1.0, 0.0
+        )
+    pick_c = sel_c[...].astype(bf16)
+    pick_r = sel_r[...].astype(bf16)
+    pack_hi, pack_lo = split(row_pack[...])
+    send_r[...] = (mm(pick_r, pack_hi) + mm(pick_r, pack_lo)).reshape(tiers, rw, levels)
+    for c in range(2):
+        packed = mm_nt(pick_c, col_acc[c].astype(bf16)) + mm_nt(
+            pick_c, col_acc[2 + c].astype(bf16)
+        )
+        send_c[:, :, c * rows : (c + 1) * rows] = packed.reshape(tiers, cw, rows)
+
+    def pack_start(i, carry):
+        send(send_r, recv_r, r_send, r_recv, i).start()
+        send(send_c, recv_c, c_send, c_recv, i).start()
+        return carry
+
+    lax.fori_loop(1, tiers, pack_start, 0)
+    recv_c[me] = send_c[me]
+    recv_r[me] = send_r[me]
+
     row_start = sy * rows
     bands_pad[...] = jnp.zeros_like(bands_pad)
     bands_pad[0 : edge + 1, :] = bands_ref[...]
@@ -338,38 +370,6 @@
         halo_h = jnp.where(low, low_bands[o : o + 1, :128], halo_h)
         halo_h = jnp.where(high, above[o : o + 1, :128], halo_h)
     halo_h = halo_h[:, : 2 * edge]
-
-    def req_wait(i, carry):
-        receive(req_ref, req_in, req_send, req_recv, i).wait_recv()
-        return carry
-
-    lax.fori_loop(1, tiers, req_wait, 0)
-    codes = jnp.transpose(req_in[:, 0, :])
-    lane_c = lax.broadcasted_iota(jnp.int32, (cw, sel_c.shape[1]), 1).astype(f32)
-    lane_r = lax.broadcasted_iota(jnp.int32, (rw, sel_r.shape[1]), 1).astype(f32)
-    for t in range(tiers):
-        sel_c[t * cw : (t + 1) * cw, :] = jnp.where(codes[0:cw, t : t + 1] == lane_c, 1.0, 0.0)
-        sel_r[t * rw : (t + 1) * rw, :] = jnp.where(
-            codes[cw : cw + rw, t : t + 1] == lane_r, 1.0, 0.0
-        )
-    pick_c = sel_c[...].astype(bf16)
-    pick_r = sel_r[...].astype(bf16)
-    pack_hi, pack_lo = split(row_pack[...])
-    send_r[...] = (mm(pick_r, pack_hi) + mm(pick_r, pack_lo)).reshape(tiers, rw, levels)
-    for c in range(2):
-        packed = mm_nt(pick_c, col_acc[c].astype(bf16)) + mm_nt(
-            pick_c, col_acc[2 + c].astype(bf16)
-        )
-        send_c[:, :, c * rows : (c + 1) * rows] = packed.reshape(tiers, cw, rows)
-
-    def pack_start(i, carry):
-        send(send_r, recv_r, r_send, r_recv, i).start()
-        send(send_c, recv_c, c_send, c_recv, i).start()
-        return carry
-
-    lax.fori_loop(1, tiers, pack_start, 0)
-    recv_c[me] = send_c[me]
-    recv_r[me] = send_r[me]
 
     @pl.when(sy > 0)
     def _():

time: 30.6 us -> 29.6 us (0.967)
  Pallas kernels: 29.6 us -> 28.8 us
    pallas_call x1, Pallas kernels: 24.3 us -> 23.5 us  [shards(): pl.pallas_call(functools.partial(exchange_kernel, (tiers, systems, slots,...]
where the time goes in v4:
time: 29.6 us; the launch traced here: 29.4 us
  Pallas kernels  28.8 us (97%)
  between operations  0.64 us (2%)
    pallas_call x1, Pallas kernels, shards(): pl.pallas_call(functools.partial(exchange_kernel, (tiers, systems, slots,...  23.5 us
    pallas_call x1, Pallas kernels, shards(): pl.pallas_call(finish_kernel, grid=(planes,), out_shape=(jax.ShapeDtypeSt...  5.3 us

profile of v4, /device:TPU:11, one launch (start us, length us, event | category | flops | bytes accessed | tf_op | source)
XLA Modules:
  0.0 29.4 jit_solution(4269047560574324314)
XLA Ops:
  0.6 23.5 %exchange.1 = (f32[8,256,512]{2,1,0:T(8,128)S(1)}, f32[8,256,512]{2,1,0:T(8,128)S(1)}, f32[128,256]{1,0:T(8,128)S(1)}, f32[128,512]{1,0:T(8,128)S(1)}, f32[16,512]{1,0:T(8,128)S(1)}, /*index=5*/f32[16,256]{1,0:T(8,128)S(1)}) custom-call(s32[4,4,24]{2,1,0:T(4,128)} %links_hbm.1, s32[16]{0:T(128)} %counts_hbm.1, s32[12]{0:T(128)} %site_hbm.1, ...), custom_call_target="tpu_custom_call" | custom-call | tf_op jit(solution)/shard_map/exchange/pallas_call | solution.py:520
  24.1 5.3 %finish.1 = (f32[8,256,512]{2,1,0:T(8,128)}, f32[8,256,512]{2,1,0:T(8,128)}) custom-call(f32[16,512]{1,0:T(8,128)S(1)} %get-tuple-element.10.spread_ref, f32[16,256]{1,0:T(8,128)S(1)} %get-tuple-element.11.row_at_ref, f32[128,256]{1,0:T(8,128)S(1)} %get-tuple-element.12.c_ref, f32[128,512]{1,0:T(8,128)S(1)} %get-tuple-element.13.r_ref, ...), custom_call_target="tpu_custom_call" | custom-call | tf_op jit(solution)/shard_map/finish/pallas_call | solution.py:577
